TPU v7x, 256 devices: a whole 4x4x8 slice. The times are simulated.
256 devices in a mesh: branch: 8 (over z), mp: 8 (over y_lo, x), dp: 4 (over y_hi, core).
Axes of the slice: x: 4, y: 4 (y_hi: 2, y_lo: 2; y = y_hi * 2 + y_lo), z: 8, core: 2. Of those that a mesh axis runs over, the one named last changes fastest.
Arguments:
- context: bfloat16 [4096, 4096], P(('branch', 'dp'), 'mp'), may hold values from -6 to 6
- residual: bfloat16 [4096, 4096], P(('branch', 'dp')), may hold values from -12 to 12
- attn_weight: bfloat16 [8, 4096, 4096], P('branch', 'mp', 'dp'), may hold values from -0.25 to 0.25
- norm_gain: bfloat16 [4096], replicated, may hold values from 0.099609375 to 1.8984375
- gate_weight: bfloat16 [8, 4096, 5504], P('branch', None, ('mp', 'dp')), may hold values from -0.09375 to 0.09375
- up_weight: bfloat16 [8, 4096, 5504], P('branch', None, ('mp', 'dp')), may hold values from -0.09375 to 0.09375
- down_weight: bfloat16 [8, 5504, 4096], P('branch', ('mp', 'dp')), may hold values from -0.078125 to 0.078125
- cotangent: bfloat16 [4096, 4096], P(('branch', 'dp')), may hold values from -0.796875 to 0.796875
- expert_ids: int32 [4096, 2], P(('branch', 'dp')), may hold values from 0 to 7, as said below
- gate_fixed: int32 [4096, 2], P(('branch', 'dp')), may hold values from 1 to 32767, as said below
Outputs:
- grad_gate: bfloat16 [8, 4096, 5504], P('branch', None, ('mp', 'dp'))
- grad_up: bfloat16 [8, 4096, 5504], P('branch', None, ('mp', 'dp'))
- grad_down: bfloat16 [8, 5504, 4096], P('branch', ('mp', 'dp'))
Inputs may be any that keep to these rules, and one draw needn't show every extreme that they name: `expert_ids`: the two entries of a row differ; in every aligned block of 128 rows some expert is named by more than 40 choices. `gate_fixed`: the two entries of a row sum to 32768.
All inputs are finite; a program needn't handle non-finite values.
Results may differ from a plain program's by a relative error of at most 0.025.
Values may be sent and summed in bfloat16 or wider, within the bound.
A program may use at most 128 MiB of HBM per device.

v0:
```python
import functools

import jax
import jax.numpy as jnp
from jax import lax
from jax.sharding import PartitionSpec as P


def slot_positions(id_block, capacity, experts):
    rows = id_block.shape[0]
    picks = jnp.concatenate([id_block[:, 0], id_block[:, 1]], axis=0)
    onehot = (picks[:, None] == jnp.arange(experts, dtype=jnp.int32)[None, :]).astype(jnp.int32)
    position = jnp.sum((jnp.cumsum(onehot, axis=0) - 1) * onehot, axis=1)
    position = jnp.where(position < capacity, position, -1)
    return jnp.stack([position[:rows], position[rows:]], axis=1)


def expert_pass(weight_set, totals, block_rows, first_row):
    w_gate, w_up, w_down = weight_set
    tokens_in, cotan_rows = block_rows
    pre_gate = jnp.dot(tokens_in, w_gate, preferred_element_type=jnp.float32)
    pre_up = jnp.dot(tokens_in, w_up, preferred_element_type=jnp.float32)
    sigmoid_gate = jax.nn.sigmoid(pre_gate)
    active = pre_gate * sigmoid_gate
    hidden = (active * pre_up).astype(jnp.bfloat16)
    back_grad = lax.dot_general(
        cotan_rows, w_down, (((1,), (1,)), ((), ())), preferred_element_type=jnp.float32
    )
    d_gate = (back_grad * pre_up * sigmoid_gate * (1.0 + pre_gate * (1.0 - sigmoid_gate))).astype(
        jnp.bfloat16
    )
    d_up = (back_grad * active).astype(jnp.bfloat16)
    contract = (((0,), (0,)), ((), ()))
    sum_gate = lax.dot_general(tokens_in, d_gate, contract, preferred_element_type=jnp.float32)
    sum_up = lax.dot_general(tokens_in, d_up, contract, preferred_element_type=jnp.float32)
    sum_down = lax.dot_general(hidden, cotan_rows, contract, preferred_element_type=jnp.float32)
    return (sum_gate, sum_up, sum_down)


def per_device(
    context,
    residual,
    attn_weight,
    norm_gain,
    gate_weight,
    up_weight,
    down_weight,
    cotangent,
    expert_ids,
    gate_fixed,
):
    branches = lax.axis_size("branch")
    summed = lax.psum(attn_weight[0].astype(jnp.float32).astype(jnp.bfloat16), "branch").astype(
        jnp.float32
    )
    merged = (summed / branches).astype(jnp.bfloat16)
    partial_out = jnp.dot(
        context,
        lax.all_gather(merged, "dp", axis=1, tiled=True),
        preferred_element_type=jnp.float32,
    ).astype(jnp.bfloat16)
    attention = lax.psum(partial_out.astype(jnp.float32).astype(jnp.bfloat16), "mp").astype(
        jnp.float32
    )
    mixed_in = residual.astype(jnp.float32) + attention
    inv_rms = lax.rsqrt(jnp.mean(mixed_in * mixed_in, axis=1, keepdims=True) + 1e-05)
    normed = (mixed_in * inv_rms * norm_gain.astype(jnp.float32)[None, :]).astype(jnp.bfloat16)
    model_width = residual.shape[1]
    group_tokens = residual.shape[0]
    experts = branches * gate_weight.shape[0]
    capacity = 5 * group_tokens // (2 * experts)
    slots = slot_positions(expert_ids, capacity, experts)
    slot_share = capacity // lax.axis_size("mp")
    offset = lax.axis_index("mp") * slot_share
    local_slot = slots - offset
    in_share = (slots >= 0) & (local_slot >= 0) & (local_slot < slot_share)
    slot_code = jnp.where(in_share, expert_ids * slot_share + local_slot, -1)
    target = jnp.arange(experts * slot_share, dtype=jnp.int32)
    matches = slot_code[None, :, :] == target[:, None, None]
    selector = jnp.any(matches, axis=2).astype(jnp.bfloat16)
    row_gate = jnp.sum(
        jnp.where(matches, gate_fixed[None, :, :].astype(jnp.float32) / 32768.0, 0.0), axis=(1, 2)
    )
    send_in = jnp.dot(selector, normed, preferred_element_type=jnp.float32).astype(jnp.bfloat16)
    send_in = send_in.reshape(experts, slot_share, model_width)
    cot_rows = jnp.dot(selector, cotangent, preferred_element_type=jnp.float32)
    send_cot = (
        (cot_rows * row_gate[:, None])
        .astype(jnp.bfloat16)
        .reshape(experts, slot_share, model_width)
    )
    hidden_width = gate_weight.shape[2]
    start_totals = (
        jnp.zeros((model_width, hidden_width), jnp.float32),
        jnp.zeros((model_width, hidden_width), jnp.float32),
        jnp.zeros((hidden_width, model_width), jnp.float32),
    )
    accumulate = functools.partial(expert_pass, (gate_weight[0], up_weight[0], down_weight[0]))
    routed_in, routed_cot = (
        lax.all_to_all(send_in, "branch", split_axis=0, concat_axis=1, tiled=True),
        lax.all_to_all(send_cot, "branch", split_axis=0, concat_axis=1, tiled=True),
    )
    totals = accumulate(
        start_totals,
        (
            lax.all_gather(routed_in[0], ("mp", "dp"), axis=0, tiled=True),
            lax.all_gather(routed_cot[0], ("mp", "dp"), axis=0, tiled=True),
        ),
        jnp.int32(0),
    )
    grad_gate = totals[0].astype(jnp.bfloat16)[None]
    grad_up = totals[1].astype(jnp.bfloat16)[None]
    grad_down = totals[2].astype(jnp.bfloat16)[None]
    return (grad_gate, grad_up, grad_down)


def solution(mesh):
    return jax.shard_map(
        per_device,
        mesh=mesh,
        in_specs=(
            P(("branch", "dp"), "mp"),
            P(("branch", "dp"), None),
            P("branch", "mp", "dp"),
            P(),
            P("branch", None, ("mp", "dp")),
            P("branch", None, ("mp", "dp")),
            P("branch", ("mp", "dp"), None),
            P(("branch", "dp"), None),
            P(("branch", "dp"), None),
            P(("branch", "dp"), None),
        ),
        out_specs=(
            P("branch", None, ("mp", "dp")),
            P("branch", None, ("mp", "dp")),
            P("branch", ("mp", "dp"), None),
        ),
        check_vma=False,
    )
```

profile of v0, /device:TPU:32, one launch (start us, length us, event | category | flops | bytes accessed | tf_op | source)
XLA Modules:
  0.0 352.5 jit_solution(13398183778796547387)
XLA Ops:
  8.0 0.0 copy-start
  8.0 0.0 all-reduce.3.cloned.1.call-start
  8.1 0.7 all-reduce.3.cloned.1.call-update
  8.7 0.0 all-gather.4.cloned.1.call-start
  8.8 80.7 %all-reduce.3.cloned.1.call-done = bf16[512,1024]{1,0:T(8,128)(2,1)} async-done(((bf16[512,1024]{1,0:T(8,128)(2,1)}), bf16[512,1024]{1,0:T(8,128)(2,1)}) %all-reduce.3.cloned.1.call-update) | async-done | bytes 1048592 | tf_op jit(solution)/shard_map/psum | solution.py:53
  89.5 2.4 multiply_convert_fusion.1
  91.9 0.0 all-gather.4.cloned.1.call-update
  92.0 0.0 all-reduce.5.cloned.1.call-start
  92.1 0.6 reduce-window.6
  92.6 0.2 slice_reduce_fusion
  92.9 0.1 fusion.18
  93.1 0.0 copy-start.2
  93.1 38.8 %all-gather.4.cloned.1.call-done = bf16[512,4096]{1,0:T(8,128)(2,1)} async-done(((bf16[512,1024]{1,0:T(8,128)(2,1)}), bf16[512,4096]{1,0:T(8,128)(2,1)}) %all-gather.4.cloned.1.call-update) | async-done | bytes 4194320 | tf_op jit(solution)/shard_map/all_gather | solution.py:59
  131.9 4.5 %fusion.3 = bf16[128,4096]{0,1:T(8,128)(2,1)} fusion(bf16[512,4096]{1,0:T(8,128)(2,1)} %all-gather.4.cloned.1.call-done, bf16[128,512]{1,0:T(8,128)(2,1)S(1)} %copy-done.4), kind=kOutput, calls=%fused_computation.7 | convolution fusion | flops 537395200 | bytes 5373952 | tf_op jit(solution)/shard_map/dot_general | solution.py:57
  136.4 0.0 all-reduce.5.cloned.1.call-update
  136.4 0.0 all-gather.8.cloned.1.call-start
  136.5 0.1 select_reduce_fusion
  136.6 0.0 copy-start.6
  136.6 0.3 fusion.4
  136.9 0.0 copy-start.3
  136.9 0.1 reshape.54
  137.0 23.9 %all_to_all.8 = bf16[8,5,4096]{2,1,0:T(8,128)(2,1)S(1)} all-to-all(bf16[8,5,4096]{2,1,0:T(8,128)(2,1)S(1)} %reshape.54), channel_id=1, replica_groups=mesh['branch'=8,'mp'=8,'dp'=4] {'branch'}, dimensions={0} | all-to-all | bytes 655360 | tf_op jit(solution)/shard_map/all_to_all | solution.py:101
  160.9 0.9 squeeze.28
  161.7 0.0 all-gather.8.cloned.1.call-update
  161.8 0.0 all-gather.6.cloned.1.call-start
  161.8 0.6 convert_element_type.69
  162.4 0.7 copy.19
  163.1 0.0 copy-start.5
  163.1 63.6 %all-reduce.5.cloned.1.call-done = bf16[128,4096]{0,1:T(8,128)(2,1)} async-done(((bf16[128,4096]{0,1:T(8,128)(2,1)}), bf16[128,4096]{0,1:T(8,128)(2,1)}) %all-reduce.5.cloned.1.call-update) | async-done | bytes 1048592 | tf_op jit(solution)/shard_map/psum | solution.py:62
  226.7 1.9 multiply_reduce_fusion
  228.6 1.0 convolution_convert_fusion.4
  229.6 0.1 reshape.53
  229.8 21.8 %all_to_all.9 = bf16[8,5,4096]{2,1,0:T(8,128)(2,1)S(1)} all-to-all(bf16[8,5,4096]{2,1,0:T(8,128)(2,1)S(1)} %reshape.53), channel_id=1, replica_groups=mesh['branch'=8,'mp'=8,'dp'=4] {'branch'}, dimensions={0} | all-to-all | bytes 655360 | tf_op jit(solution)/shard_map/all_to_all | solution.py:100
  251.6 0.9 squeeze.27
  252.5 0.0 all-gather.6.cloned.1.call-update
  252.5 0.0 copy-start.9
  252.5 0.0 all-gather.8.cloned.1.call-done
  252.6 8.6 %fusion.9 = f32[1280,172]{0,1:T(8,128)} fusion(bf16[1280,4096]{1,0:T(8,128)(2,1)} %all-gather.8.cloned.1.call-done, bf16[1,172,4096]{2,1,0:T(8,128)(2,1)S(1)} %copy-done), kind=kOutput, calls=%fused_computation.19 | convolution fusion | flops 1803550720 | bytes 12775424 | tf_op jit(solution)/shard_map/dot_general | solution.py:26
  261.2 58.5 %all-gather.6.cloned.1.call-done = bf16[1280,4096]{1,0:T(8,128)(2,1)} async-done(((bf16[40,4096]{1,0:T(8,128)(2,1)}), bf16[1280,4096]{1,0:T(8,128)(2,1)}) %all-gather.6.cloned.1.call-update) | async-done | bytes 10485776 | tf_op jit(solution)/shard_map/all_gather | solution.py:106
  319.7 7.8 %fusion.5 = f32[1280,172]{0,1:T(8,128)S(1)} fusion(bf16[1280,4096]{1,0:T(8,128)(2,1)} %all-gather.6.cloned.1.call-done, bf16[1,4096,172]{1,2,0:T(8,128)(2,1)S(1)} %copy-done.9), kind=kOutput, calls=%fused_computation.15 | convolution fusion | flops 1803550720 | bytes 12775424 | tf_op jit(solution)/shard_map/dot_general | solution.py:21
  327.5 0.0 slice-start.2
  327.5 0.0 slice-start.3
  327.5 7.8 %fusion.7 = f32[1280,172]{0,1:T(8,128)S(1)} fusion(bf16[1280,4096]{1,0:T(8,128)(2,1)} %all-gather.6.cloned.1.call-done, bf16[1,4096,172]{1,2,0:T(8,128)(2,1)S(1)} %copy-done.10), kind=kOutput, calls=%fused_computation.17 | convolution fusion | flops 1803550720 | bytes 12775424 | tf_op jit(solution)/shard_map/dot_general | solution.py:22
  335.3 0.0 slice-start.5
  335.3 0.0 copy-start.11
  335.3 3.2 fusion.2
  338.6 3.5 %fusion = bf16[1,4096,172]{1,2,0:T(8,128)(2,1)} fusion(bf16[1280,4096]{1,0:T(8,128)(2,1)S(1)} %bitcast.49, f32[1280,172]{0,1:T(8,128)S(1)} %fusion.5, f32[1280,172]{0,1:T(8,128)S(1)} %copy-done.11, f32[1280,172]{0,1:T(8,128)S(1)} %fusion.7), kind=kOutput, calls=%fused_computation.4 | convolution fusion | flops 1806456832 | bytes 14536704 | tf_op jit(solution)/shard_map/dot_general | solution.py:34
  342.1 3.3 fusion.1
  (39 shorter events, 0.2 us)
Async XLA Ops:
  8.0 244.6 %copy-start = (bf16[1,172,4096]{2,1,0:T(8,128)(2,1)S(1)}, bf16[1,172,4096]{2,1,0:T(8,128)(2,1)}, u32[]{:S(2)}) copy-start(bf16[1,172,4096]{2,1,0:T(8,128)(2,1)} %param.16) | copy-start | bytes 4227076
  8.0 81.5 %all-reduce.3.cloned.1.call-start = ((), (), s32[]{:S(2)}) async-start(), calls=%async_computation.2 | async-start | bytes 2097152 | tf_op jit(solution)/shard_map/psum | solution.py:53
  8.1 83.9 %copy-start.7 = (s32[128,2]{0,1:T(2,128)S(1)}, s32[128,2]{0,1:T(2,128)}, u32[]{:S(2)}) copy-start(s32[128,2]{0,1:T(2,128)} %param.18) | copy-start | bytes 3076
  8.1 84.9 %copy-start.8 = (s32[128,2]{0,1:T(2,128)S(1)}, s32[128,2]{0,1:T(2,128)}, u32[]{:S(2)}) copy-start(s32[128,2]{0,1:T(2,128)} %param.19) | copy-start | bytes 3076
  8.1 123.8 %copy-start.4 = (bf16[128,512]{1,0:T(8,128)(2,1)S(1)}, bf16[128,512]{1,0:T(8,128)(2,1)}, u32[]{:S(2)}) copy-start(bf16[128,512]{1,0:T(8,128)(2,1)} %param.10) | copy-start | bytes 393220
  8.7 123.1 %all-gather.4.cloned.1.call-start = ((), (), s32[]{:S(2)}) async-start(), calls=%async_computation.3 | async-start | bytes 5242880 | tf_op jit(solution)/shard_map/all_gather | solution.py:59
  92.0 134.7 %all-reduce.5.cloned.1.call-start = ((), (), s32[]{:S(2)}) async-start(), calls=%async_computation.4 | async-start | bytes 2097152 | tf_op jit(solution)/shard_map/psum | solution.py:62
  93.1 43.5 %copy-start.2 = (bf16[128,4096]{1,0:T(8,128)(2,1)S(1)}, bf16[128,4096]{1,0:T(8,128)(2,1)}, u32[]{:S(2)}) copy-start(bf16[128,4096]{1,0:T(8,128)(2,1)} %param.17) | copy-start | bytes 3145732
  136.4 116.2 %all-gather.8.cloned.1.call-start = ((), (), s32[]{:S(2)}) async-start(), calls=%async_computation.6 | async-start | bytes 10813440 | tf_op jit(solution)/shard_map/all_gather | solution.py:107
  136.6 25.3 %copy-start.6 = (bf16[4096]{0:T(1024)(128)(2,1)S(1)}, bf16[4096]{0:T(1024)(128)(2,1)}, u32[]{:S(2)}) copy-start(bf16[4096]{0:T(1024)(128)(2,1)} %param.13) | copy-start | bytes 24580
  136.9 25.6 %copy-start.3 = (bf16[128,4096]{1,0:T(8,128)(2,1)S(1)}, bf16[128,4096]{1,0:T(8,128)(2,1)}, u32[]{:S(2)}) copy-start(bf16[128,4096]{1,0:T(8,128)(2,1)} %param.11) | copy-start | bytes 3145732
  161.8 157.9 %all-gather.6.cloned.1.call-start = ((), (), s32[]{:S(2)}) async-start(), calls=%async_computation.5 | async-start | bytes 10813440 | tf_op jit(solution)/shard_map/all_gather | solution.py:106
  163.1 65.5 %copy-start.5 = (f32[4096]{0:T(1024)S(1)}, f32[4096]{0:T(1024)}, u32[]{:S(2)}) copy-start(f32[4096]{0:T(1024)} %convert_element_type.69) | copy-start | bytes 49156
  226.7 1.9 copy-start.1
  252.5 67.2 %copy-start.9 = (bf16[1,4096,172]{1,2,0:T(8,128)(2,1)S(1)}, bf16[1,4096,172]{1,2,0:T(8,128)(2,1)}, u32[]{:S(2)}) copy-start(bf16[1,4096,172]{1,2,0:T(8,128)(2,1)} %param.14) | copy-start | bytes 4227076
  319.7 7.8 %copy-start.10 = (bf16[1,4096,172]{1,2,0:T(8,128)(2,1)S(1)}, bf16[1,4096,172]{1,2,0:T(8,128)(2,1)}, u32[]{:S(2)}) copy-start(bf16[1,4096,172]{1,2,0:T(8,128)(2,1)} %param.15) | copy-start | bytes 4227076
  319.7 15.6 %slice-start = ((s8[10485760]{0:T(1024)(128)(4,1)}), s8[4194304]{0:T(1024)(128)(4,1)S(1)}, s32[]{:S(2)}) async-start(s8[10485760]{0:T(1024)(128)(4,1)} %bitcast.46), calls=%async_computation.7 | async-start | bytes 8388608
  319.7 15.6 %slice-start.1 = ((s8[10485760]{0:T(1024)(128)(4,1)}), s8[4194304]{0:T(1024)(128)(4,1)S(1)}, s32[]{:S(2)}) async-start(s8[10485760]{0:T(1024)(128)(4,1)} %bitcast.46), calls=%async_computation.8 | async-start | bytes 8388608
  327.5 7.8 %slice-start.2 = ((s8[10485760]{0:T(1024)(128)(4,1)}), s8[2097152]{0:T(1024)(128)(4,1)S(1)}, s32[]{:S(2)}) async-start(s8[10485760]{0:T(1024)(128)(4,1)} %bitcast.46), calls=%async_computation.9 | async-start | bytes 4194304
  327.5 11.1 %slice-start.3 = ((s8[10485760]{0:T(1024)(128)(4,1)}), s8[4194304]{0:T(1024)(128)(4,1)S(1)}, s32[]{:S(2)}) async-start(s8[10485760]{0:T(1024)(128)(4,1)} %bitcast.48), calls=%async_computation.10 | async-start | bytes 8388608
  327.5 11.1 %slice-start.4 = ((s8[10485760]{0:T(1024)(128)(4,1)}), s8[4194304]{0:T(1024)(128)(4,1)S(1)}, s32[]{:S(2)}) async-start(s8[10485760]{0:T(1024)(128)(4,1)} %bitcast.48), calls=%async_computation.11 | async-start | bytes 8388608
  335.3 3.3 slice-start.5
  335.3 3.3 copy-start.11
Sparse Core Ops, SparseCore 0:
  11.2 78.3 all-reduce.2
  92.1 39.7 all-gather.3
  136.5 90.1 all-reduce.4
Sparse Core Ops, SparseCore 1:
  161.9 76.8 all-gather.7
  252.6 67.0 all-gather.5
where the time goes:
time: 354 us; the launch traced here: 353 us
  waiting for transfers between devices  242 us (68%)
  blocking collectives  45.7 us (13%)
  matrix products  40 us (11%)
  between operations  15.5 us (4%)
  other arithmetic  5.8 us (2%)
    psum x1, waiting for transfers between devices, per_device(): lax.psum(attn_weight[0].astype(jnp.float32).astype(jnp.bfloat16), 'branch')  80.7 us
    psum x1, waiting for transfers between devices, per_device(): lax.psum(partial_out.astype(jnp.float32).astype(jnp.bfloat16), 'mp')  63.6 us
    all_gather x1, waiting for transfers between devices, per_device(): lax.all_gather(routed_in[0], ('mp', 'dp'), axis=0, tiled=True)  58.5 us
    all_gather x1, waiting for transfers between devices, per_device(): lax.all_gather(merged, 'dp', axis=1, tiled=True)  38.8 us
    all_to_all x1, blocking collectives, per_device(): lax.all_to_all(send_cot, 'branch', split_axis=0, concat_axis=1, tiled=True)  23.9 us
    all_to_all x1, blocking collectives, per_device(): lax.all_to_all(send_in, 'branch', split_axis=0, concat_axis=1, tiled=True)  21.8 us
    dot_general x1, matrix products, expert_pass(): lax.dot_general(cotan_rows, w_down, (((1,), (1,)), ((), ())), preferred_e...  8.63 us
    dot_general x1, matrix products, expert_pass(): pre_up = jnp.dot(tokens_in, w_up, preferred_element_type=jnp.float32)  7.76 us
  transfers between devices with their start and end apart: 5, of which 4 were waited for; matrix products, arithmetic and copies ran while one was open for 5% of the time, Pallas kernels for 0%

commit v1 on v0

v1 whole, which is shorter than its diff:
```python
import functools

import jax
import jax.numpy as jnp
from jax import lax
from jax.experimental import pallas as pl
from jax.experimental.pallas import tpu as pltpu
from jax.sharding import PartitionSpec as P

MESH = pl.DeviceIdType.MESH
BF = jnp.bfloat16
F32 = jnp.float32
NT = (((1,), (1,)), ((), ()))


def slot_positions(id_block, capacity, experts):
    rows = id_block.shape[0]
    picks = jnp.concatenate([id_block[:, 0], id_block[:, 1]], axis=0)
    onehot = (picks[:, None] == jnp.arange(experts, dtype=jnp.int32)[None, :]).astype(jnp.int32)
    position = jnp.sum((jnp.cumsum(onehot, axis=0) - 1) * onehot, axis=1)
    position = jnp.where(position < capacity, position, -1)
    return jnp.stack([position[:rows], position[rows:]], axis=1)


class Coords:
    def __init__(self):
        self.z = lax.axis_index("branch")
        self.mp = lax.axis_index("mp")
        self.dp = lax.axis_index("dp")
        self.x = lax.rem(self.mp, 4)
        self.core = lax.rem(self.dp, 2)
        self.y = lax.div(self.dp, 2) * 2 + lax.div(self.mp, 4)

    def at(self, da, db, core):
        other = 1 - core
        x = lax.rem(self.x + other * da + core * db + 8, 4)
        y = lax.rem(self.y + core * da + other * db + 8, 4)
        return x, y

    def device(self, da, db):
        x, y = self.at(da, db, self.core)
        return (self.z, lax.rem(y, 2) * 4 + x, lax.div(y, 2) * 2 + self.core)

    def piece(self, da, db, core=None):
        core = self.core if core is None else core
        x, y = self.at(da, db, core)
        return (lax.div(y, 2) * 2 + core) * 8 + lax.rem(y, 2) * 4 + x

    def sibling(self):
        return (self.z, self.mp, self.dp + 1 - 2 * self.core)


RING = (0, -1, 1, 2)


class PlaneGather:
    COPIES = 36

    def __init__(self, at, buf, send, recv):
        self.at, self.buf, self.send, self.recv = at, buf, send, recv
        self.half = buf.shape[1] // 2
        self.sent = []

    def view(self, piece, half=None):
        if half is None:
            return self.buf.at[piece]
        return self.buf.at[piece, pl.ds(half * self.half, self.half)]

    def copy(self, index, piece, device, half=None):
        ref = self.view(piece, half)
        return pltpu.make_async_remote_copy(
            src_ref=ref,
            dst_ref=ref,
            send_sem=self.send.at[index],
            recv_sem=self.recv.at[index],
            device_id=device,
            device_id_type=MESH,
        )

    def go(self, index, piece, device, half=None):
        descriptor = self.copy(index, piece, device, half)
        descriptor.start()
        self.sent.append(descriptor)

    def arrived(self, index, piece, half=None):
        self.copy(index, piece, self.at.sibling(), half).wait_recv()

    def to_sibling(self, qa, qb):
        index = 20 + 4 * RING.index(qa) + RING.index(qb)
        self.go(index, self.at.piece(qa, qb), self.at.sibling())

    def spread(self, qa):
        index = 4 + 4 * RING.index(qa)
        piece = self.at.piece(qa, 0)
        self.go(index, piece, self.at.device(0, 1))
        self.go(index + 1, piece, self.at.device(0, -1))
        self.to_sibling(qa, 0)

    def start(self):
        piece = self.at.piece(0, 0)
        self.go(0, piece, self.at.device(1, 0))
        self.go(1, piece, self.at.device(-1, 0))
        self.spread(0)

    def first_axis(self):
        low, high = self.at.piece(-1, 0), self.at.piece(1, 0)
        self.arrived(0, low)
        self.go(2, low, self.at.device(1, 0), 0)
        self.arrived(1, high)
        self.go(3, high, self.at.device(-1, 0), 1)
        self.spread(-1)
        self.spread(1)

    def first_axis_far(self):
        far = self.at.piece(2, 0)
        self.arrived(2, far, 0)
        self.arrived(3, far, 1)
        self.spread(2)

    def relay(self, qa):
        index = 4 + 4 * RING.index(qa)
        low, high = self.at.piece(qa, -1), self.at.piece(qa, 1)
        self.arrived(index, low)
        self.go(index + 2, low, self.at.device(0, 1), 0)
        self.arrived(index + 1, high)
        self.go(index + 3, high, self.at.device(0, -1), 1)
        self.to_sibling(qa, -1)
        self.to_sibling(qa, 1)

    def far(self, qa):
        index = 4 + 4 * RING.index(qa)
        piece = self.at.piece(qa, 2)
        self.arrived(index + 2, piece, 0)
        self.arrived(index + 3, piece, 1)
        self.to_sibling(qa, 2)

    def from_sibling(self, qa):
        for qb in RING:
            index = 20 + 4 * RING.index(qa) + RING.index(qb)
            self.arrived(index, self.at.piece(qa, qb, 1 - self.at.core))

    def own_group(self, qa):
        return [self.at.piece(qa, qb) for qb in RING]

    def sibling_group(self, qa):
        return [self.at.piece(qa, qb, 1 - self.at.core) for qb in RING]

    def steps(self):
        return [
            self.start,
            self.first_axis,
            functools.partial(self.relay, 0),
            self.first_axis_far,
            functools.partial(self.relay, -1),
            functools.partial(self.relay, 1),
            functools.partial(self.far, 0),
            functools.partial(self.relay, 2),
            functools.partial(self.far, -1),
            functools.partial(self.far, 1),
            functools.partial(self.far, 2),
        ]

    def finish(self):
        for descriptor in self.sent:
            descriptor.wait_send()


def kernel(
    attn_ref, context_ref, residual_ref, cot_ref, info_ref, gain_ref, wg_ref, wu_ref, wd_ref,
    og_ref, ou_ref, od_ref,
    rows_in, rows_cot, ctx_all, wgu, wd, wtmp, acc, acc_back, ssq, dgu, hid,
    red_in_p, red_in_m, red_out_p, red_out_m, red_sum, merged_all,
    res_all, cot_all, info_all, sel, route_x, route_c,
    w_sem, in_send, in_recv, in_local, cot_send, cot_recv, ctx_send, ctx_recv,
    ex_send, ex_recv, ex_local, rp_send, rp_recv, rm_send, rm_recv,
    ma_send, ma_recv, ga_send, ga_recv, tx_send, tx_recv, tc_send, tc_recv,
):
    at = Coords()
    z, mp, dp = at.z, at.mp, at.dp
    own = at.piece(0, 0)
    hidden = wg_ref.shape[0]
    hid_pad = wgu.shape[0] // 2
    pending = []

    def z_dev(k):
        return (lax.rem(z + k + 8, 8), mp, dp)

    def mp_dev(k):
        return (z, lax.rem(mp + k, 8), dp)

    def dp_dev(k):
        return (z, mp, lax.rem(dp + k, 4))

    def remote(src, dst, send, recv, device):
        return pltpu.make_async_remote_copy(
            src_ref=src, dst_ref=dst, send_sem=send, recv_sem=recv,
            device_id=device, device_id_type=MESH,
        )

    def push(src, dst, send, recv, device):
        descriptor = remote(src, dst, send, recv, device)
        descriptor.start()
        pending.append(descriptor)

    def landed(dst, recv, send):
        remote(dst, dst, send, recv, at.sibling()).wait_recv()

    barrier = pltpu.get_barrier_semaphore()
    peers = [z_dev(k) for k in range(1, 8)] + [mp_dev(k) for k in range(1, 8)]
    peers += [dp_dev(k) for k in range(1, 4)]
    for dy in (1, -1):
        y = lax.rem(at.y + dy + 4, 4)
        peers.append((z, lax.rem(y, 2) * 4 + at.x, lax.div(y, 2) * 2 + at.core))
    for peer in peers:
        pl.semaphore_signal(barrier, inc=1, device_id=peer, device_id_type=MESH)

    weights = [
        pltpu.make_async_copy(wg_ref, wtmp.at[0], w_sem.at[0]),
        pltpu.make_async_copy(wu_ref, wtmp.at[1], w_sem.at[1]),
        pltpu.make_async_copy(wd_ref, wd, w_sem.at[2]),
    ]
    ctx_copy = pltpu.make_async_copy(context_ref, ctx_all.at[own], in_local.at[0])
    ctx_copy.start()
    dp_rows = pl.ds(pl.multiple_of(dp * 128, 128), 128)

    def columns(k):
        d = lax.rem(dp + k, 4)
        return pl.ds(pl.multiple_of(d * 1024 + mp * 128, 128), 128)

    locals_ = [
        pltpu.make_async_copy(residual_ref.at[:, columns(0)], res_all.at[dp_rows], ex_local.at[0]),
        pltpu.make_async_copy(cot_ref.at[:, columns(0)], cot_all.at[dp_rows], ex_local.at[1]),
        pltpu.make_async_copy(info_ref, info_all.at[dp], ex_local.at[2]),
    ]
    for copy in locals_:
        copy.start()
    for copy in weights:
        copy.start()
    pl.semaphore_wait(barrier, len(peers))

    for k in range(1, 4):
        push(cot_ref.at[:, columns(k)], cot_all.at[dp_rows], ex_send.at[0, k], ex_recv.at[0, k], dp_dev(k))
        push(info_ref, info_all.at[dp], ex_send.at[1, k], ex_recv.at[1, k], dp_dev(k))

    def chunk(k):
        t = lax.rem(z + k + 8, 8)
        return pl.ds(pl.multiple_of(t * 64, 64), 64)

    half_cols = [pl.ds(0, 512), pl.ds(512, 512)]

    def reduce_step(step):
        for h in range(2):
            cols = half_cols[h]
            if step < 4:
                src = attn_ref.at[chunk(4), cols]
                if step > 0:
                    landed(red_in_p.at[step - 1, h], rp_recv.at[step - 1, h], rp_send.at[step - 1, h])
                    red_out_p[step - 1, h] = (
                        red_in_p[step - 1, h].astype(F32) + attn_ref[chunk(4 - step), cols].astype(F32)
                    ).astype(BF)
                    src = red_out_p.at[step - 1, h]
                push(src, red_in_p.at[step, h], rp_send.at[step, h], rp_recv.at[step, h], z_dev(1))
            if step < 3:
                src = attn_ref.at[chunk(-3), cols]
                if step > 0:
                    landed(red_in_m.at[step - 1, h], rm_recv.at[step - 1, h], rm_send.at[step - 1, h])
                    red_out_m[step - 1, h] = (
                        red_in_m[step - 1, h].astype(F32) + attn_ref[chunk(step - 3), cols].astype(F32)
                    ).astype(BF)
                    src = red_out_m.at[step - 1, h]
                push(src, red_in_m.at[step, h], rm_send.at[step, h], rm_recv.at[step, h], z_dev(-1))

    reduce_step(0)
    for k in range(1, 4):
        push(residual_ref.at[:, columns(k)], res_all.at[dp_rows], ex_send.at[2, k], ex_recv.at[2, k], dp_dev(k))

    ctx_gather = PlaneGather(at, ctx_all, ctx_send, ctx_recv)
    cot_gather = PlaneGather(at, rows_cot, cot_send, cot_recv)
    in_gather = PlaneGather(at, rows_in, in_send, in_recv)
    ctx_copy.wait()
    ctx_steps = ctx_gather.steps()
    cot_steps = cot_gather.steps()
    in_steps = in_gather.steps()
    ctx_steps.pop(0)()

    def from_group(k):
        d = lax.rem(dp - k + 4, 4)
        return pl.ds(pl.multiple_of(d * 128, 128), 128), d

    locals_[1].wait()
    locals_[2].wait()
    for k in range(1, 4):
        rows, d = from_group(k)
        landed(cot_all.at[rows], ex_recv.at[0, k], ex_send.at[0, k])
        landed(info_all.at[d], ex_recv.at[1, k], ex_send.at[1, k])

    @pl.loop(0, 8)
    def _(e):
        place = (lax.broadcasted_iota(jnp.int32, (160, 128), 0) + e * 160).astype(F32)
        row_gate = jnp.zeros((160, 1), F32)
        rows = pl.ds(pl.multiple_of(e * 160, 160), 160)
        for d in range(4):
            info = info_all[d]
            first = place == info[0:1, :]
            second = place == info[1:2, :]
            sel[rows, d * 128:(d + 1) * 128] = jnp.where(first | second, 1.0, 0.0).astype(BF)
            gates = jnp.where(first, info[2:3, :], jnp.where(second, info[3:4, :], 0.0))
            row_gate += jnp.sum(gates, axis=1, keepdims=True)
        picked = jnp.dot(sel[rows, :], cot_all[...], preferred_element_type=F32)
        route_c[e] = (picked * row_gate).astype(BF)

    own_block = pl.ds(pl.multiple_of(z * 160, 160), 160)

    def exchange(route, gathered, send, recv):
        for k in range(1, 8):
            e = lax.rem(z + k, 8)
            push(route.at[e], gathered.at[own, own_block], send.at[k], recv.at[k], z_dev(k))
        gathered[own, own_block, :] = route[z]

    def exchanged(gathered, send, recv):
        for k in range(1, 8):
            b = lax.rem(z - k + 8, 8)
            landed(gathered.at[own, pl.ds(pl.multiple_of(b * 160, 160), 160)], recv.at[k], send.at[k])

    exchange(route_c, rows_cot, tc_send, tc_recv)

    reduce_step(1)
    ctx_steps.pop(0)()
    reduce_step(2)
    ctx_steps.pop(0)()
    ctx_steps.pop(0)()
    reduce_step(3)
    ctx_steps.pop(0)()
    ctx_steps.pop(0)()

    for h in range(2):
        landed(red_in_p.at[3, h], rp_recv.at[3, h], rp_send.at[3, h])
        landed(red_in_m.at[2, h], rm_recv.at[2, h], rm_send.at[2, h])
        total = (
            red_in_p[3, h].astype(F32) + red_in_m[2, h].astype(F32)
            + attn_ref[chunk(0), half_cols[h]].astype(F32)
        )
        mean = (total * 0.125).astype(BF)
        for part in range(4):
            red_sum[4 * h + part] = mean[:, part * 128:(part + 1) * 128]
    own_rows = pl.ds(pl.multiple_of(z * 64, 64), 64)
    for k in range(1, 8):
        j = lax.rem(mp + k, 8)
        push(red_sum.at[j], merged_all.at[mp, own_rows], ma_send.at[k], ma_recv.at[k], mp_dev(k))
    merged_all[mp, own_rows, :] = red_sum[mp]
    ctx_steps.pop(0)()
    exchanged(rows_cot, tc_send, tc_recv)
    cot_steps.pop(0)()
    for k in range(1, 8):
        j = lax.rem(mp - k + 8, 8)
        landed(merged_all.at[j, own_rows], ma_recv.at[k], ma_send.at[k])

    def merged_view(k, h):
        t = lax.rem(z + k + 8, 8)
        return merged_all.at[pl.ds(4 * h, 4), pl.ds(pl.multiple_of(t * 64, 64), 64)]

    def gather_step(step):
        for h in range(2):
            if step < 5 and step > 0:
                landed(merged_view(-step, h), ga_recv.at[0, step - 1, h], ga_send.at[0, step - 1, h])
            if step < 4:
                view = merged_view(-step, h)
                push(view, view, ga_send.at[0, step, h], ga_recv.at[0, step, h], z_dev(1))
            if step < 4 and step > 0:
                landed(merged_view(step, h), ga_recv.at[1, step - 1, h], ga_send.at[1, step - 1, h])
            if step < 3:
                view = merged_view(step, h)
                push(view, view, ga_send.at[1, step, h], ga_recv.at[1, step, h], z_dev(-1))

    gather_step(0)
    for copy in weights:
        copy.wait()
    wgu[0:hidden, :] = wtmp[0]
    wgu[hid_pad:hid_pad + hidden, :] = wtmp[1]
    acc[...] = jnp.zeros_like(acc)
    acc_back[...] = jnp.zeros_like(acc_back)
    ssq[...] = jnp.zeros_like(ssq)
    while ctx_steps:
        ctx_steps.pop(0)()
    gather_step(1)
    cot_steps.pop(0)()
    gather_step(2)
    cot_steps.pop(0)()
    gather_step(3)
    cot_steps.pop(0)()
    for qa in RING:
        ctx_gather.from_sibling(qa)
    gather_step(4)
    for k in range(1, 4):
        rows, _ = from_group(k)
        landed(res_all.at[rows], ex_recv.at[2, k], ex_send.at[2, k])
    locals_[0].wait()

    own_gain = gain_ref[pl.ds(own, 1), :]

    for d in range(4):
        total = jnp.zeros((128, 128), F32)
        for j in range(8):
            total += jnp.dot(ctx_all[d * 8 + j], merged_all[j], preferred_element_type=F32)
        rows = slice(d * 128, (d + 1) * 128)
        mixed = total + res_all[rows, :].astype(F32)
        res_all[rows, :] = (mixed * own_gain).astype(BF)

    @pl.loop(0, 8)
    def _(e):
        rows = pl.ds(pl.multiple_of(e * 160, 160), 160)
        route_x[e] = jnp.dot(sel[rows, :], res_all[...], preferred_element_type=F32).astype(BF)

    exchange(route_x, rows_in, tx_send, tx_recv)
    cot_steps.pop(0)()
    cot_steps.pop(0)()
    exchanged(rows_in, tx_send, tx_recv)
    in_steps.pop(0)()
    while cot_steps:
        cot_steps.pop(0)()

    blocks = 5
    width = acc.shape[1] // blocks

    def lanes(piece):
        return pl.ds(pl.multiple_of(piece * 128, 128), 128)

    def back_group(group):
        lhs = jnp.concatenate([wd[:, lanes(p)] for p in group], axis=1)

        @pl.loop(0, blocks)
        def _(n):
            rows = pl.ds(pl.multiple_of(n * width, width), width)
            rhs = jnp.concatenate([rows_cot[p, rows, :] for p in group], axis=1)
            acc_back[:, rows] += lax.dot_general(lhs, rhs, NT, preferred_element_type=F32)

    def fore_group(group):
        lhs = jnp.concatenate([wgu[:, lanes(p)] for p in group], axis=1)
        inverse = jnp.concatenate([1.0 / gain_ref[pl.ds(p, 1), :] for p in group], axis=1)
        ones = jnp.ones((8, 512), BF)

        @pl.loop(0, blocks)
        def _(n):
            rows = pl.ds(pl.multiple_of(n * width, width), width)
            rhs = jnp.concatenate([rows_in[p, rows, :] for p in group], axis=1)
            acc[:, rows] += lax.dot_general(lhs, rhs, NT, preferred_element_type=F32)
            scaled = rhs.astype(F32) * inverse
            ssq[:, rows] += lax.dot_general(
                ones, (scaled * scaled).astype(BF), NT, preferred_element_type=F32
            )

    back_group(cot_gather.own_group(0))
    back_group(cot_gather.own_group(-1))
    in_steps.pop(0)()
    back_group(cot_gather.own_group(1))
    back_group(cot_gather.own_group(2))
    in_steps.pop(0)()
    for qa in RING[:2]:
        cot_gather.from_sibling(qa)
        back_group(cot_gather.sibling_group(qa))
    in_steps.pop(0)()
    for qa in RING[2:]:
        cot_gather.from_sibling(qa)
        back_group(cot_gather.sibling_group(qa))
    while in_steps:
        in_steps.pop(0)()
    for qa in RING:
        fore_group(in_gather.own_group(qa))
    for qa in RING:
        in_gather.from_sibling(qa)
        fore_group(in_gather.sibling_group(qa))

    @pl.loop(0, blocks)
    def _(n):
        rows = pl.ds(pl.multiple_of(n * width, width), width)
        inv = lax.rsqrt(ssq[0:1, rows] * (1.0 / 4096.0) + 1e-05)
        gate = acc[0:hidden, rows] * inv
        up = acc[hid_pad:hid_pad + hidden, rows] * inv
        back = acc_back[:, rows]
        sig = jax.nn.sigmoid(gate)
        active = gate * sig
        hid[:, rows] = (active * up).astype(BF)
        back = back * inv
        dgu[0:hidden, rows] = (back * up * sig * (1.0 + gate * (1.0 - sig))).astype(BF)
        dgu[hid_pad:hid_pad + hidden, rows] = (back * active).astype(BF)

    @pl.loop(0, 16)
    def _(n):
        cols = pl.ds(pl.multiple_of(n * 256, 256), 256)
        rhs = jnp.concatenate([rows_in[2 * n], rows_in[2 * n + 1]], axis=1)
        both = jnp.dot(dgu[...], rhs, preferred_element_type=F32).astype(BF)
        og_ref[:, cols] = both[0:hidden]
        ou_ref[:, cols] = both[hid_pad:hid_pad + hidden]
        rhs = jnp.concatenate([rows_cot[2 * n], rows_cot[2 * n + 1]], axis=1)
        od_ref[:, cols] = jnp.dot(hid[...], rhs, preferred_element_type=F32).astype(BF)

    for gather in (ctx_gather, cot_gather, in_gather):
        gather.finish()
    for descriptor in pending:
        descriptor.wait_send()


def per_device(
    context, residual, attn_weight, norm_gain, gate_weight, up_weight, down_weight,
    cotangent, expert_ids, gate_fixed,
):
    slots = slot_positions(expert_ids, 40, 8)
    code = jnp.where(slots >= 0, expert_ids * 160 + lax.axis_index("dp") * 40 + slots, -1)
    info = jnp.concatenate(
        [
            code.T.astype(jnp.float32),
            gate_fixed.T.astype(jnp.float32) / 32768.0,
            jnp.zeros((4, 128), jnp.float32),
        ],
        axis=0,
    )
    gain = norm_gain.astype(jnp.float32).reshape(32, 128)
    hidden = gate_weight.shape[2]
    pad = 176
    dma = pltpu.SemaphoreType.DMA
    vmem = pl.BlockSpec(memory_space=pltpu.VMEM)
    hbm = pl.BlockSpec(memory_space=pl.ANY)
    out = jax.ShapeDtypeStruct((hidden, 4096), BF)
    copies = PlaneGather.COPIES
    grads = pl.pallas_call(
        kernel,
        out_shape=(out, out, out),
        in_specs=[vmem, hbm, hbm, hbm, hbm, vmem, hbm, hbm, hbm],
        out_specs=(vmem, vmem, vmem),
        scratch_shapes=[
            pltpu.VMEM((32, 1280, 128), BF),
            pltpu.VMEM((32, 1280, 128), BF),
            pltpu.VMEM((32, 128, 512), BF),
            pltpu.VMEM((2 * pad, 4096), BF),
            pltpu.VMEM((hidden, 4096), BF),
            pltpu.VMEM((2, hidden, 4096), BF),
            pltpu.VMEM((2 * pad, 1280), F32),
            pltpu.VMEM((hidden, 1280), F32),
            pltpu.VMEM((8, 1280), F32),
            pltpu.VMEM((2 * pad, 1280), BF),
            pltpu.VMEM((hidden, 1280), BF),
            pltpu.VMEM((4, 2, 64, 512), BF),
            pltpu.VMEM((3, 2, 64, 512), BF),
            pltpu.VMEM((3, 2, 64, 512), BF),
            pltpu.VMEM((2, 2, 64, 512), BF),
            pltpu.VMEM((8, 64, 128), BF),
            pltpu.VMEM((8, 512, 128), BF),
            pltpu.VMEM((512, 128), BF),
            pltpu.VMEM((512, 128), BF),
            pltpu.VMEM((4, 8, 128), F32),
            pltpu.VMEM((1280, 512), BF),
            pltpu.VMEM((8, 160, 128), BF),
            pltpu.VMEM((8, 160, 128), BF),
            dma((3,)),
            dma((copies,)), dma((copies,)), dma((1,)),
            dma((copies,)), dma((copies,)),
            dma((copies,)), dma((copies,)),
            dma((3, 4)), dma((3, 4)), dma((3,)),
            dma((4, 2)), dma((4, 2)), dma((3, 2)), dma((3, 2)),
            dma((8,)), dma((8,)),
            dma((2, 4, 2)), dma((2, 4, 2)),
            dma((8,)), dma((8,)),
            dma((8,)), dma((8,)),
        ],
        compiler_params=pltpu.CompilerParams(
            collective_id=0, has_side_effects=True, vmem_limit_bytes=66 * 1000 * 1000
        ),
    )(
        attn_weight[0], context, residual, cotangent, info, gain,
        gate_weight[0].T, up_weight[0].T, down_weight[0],
    )
    return grads[0].T[None], grads[1].T[None], grads[2][None]


def solution(mesh):
    return jax.shard_map(
        per_device,
        mesh=mesh,
        in_specs=(
            P(("branch", "dp"), "mp"),
            P(("branch", "dp"), None),
            P("branch", "mp", "dp"),
            P(),
            P("branch", None, ("mp", "dp")),
            P("branch", None, ("mp", "dp")),
            P("branch", ("mp", "dp"), None),
            P(("branch", "dp"), None),
            P(("branch", "dp"), None),
            P(("branch", "dp"), None),
        ),
        out_specs=(
            P("branch", None, ("mp", "dp")),
            P("branch", None, ("mp", "dp")),
            P("branch", ("mp", "dp"), None),
        ),
        check_vma=False,
    )
```

time: 354 us -> 147 us (0.42)
  the two profiles are of different devices: /device:TPU:32 before, /device:TPU:9 now
where the time goes in v1:
time: 147 us
  Pallas kernels  136 us (93%)
  local copies, waits for them, and re-layouts  6.76 us (5%)
  other arithmetic  4.08 us (3%)
    pallas_call x1, Pallas kernels, per_device(): pl.pallas_call(kernel, out_shape=(out, out, out), in_specs=[vmem, hbm, hb...  136 us
    unnamed x7, local copies, waits for them, and re-layouts  5.7 us

profile of v1, /device:TPU:9, one launch (start us, length us, event | category | flops | bytes accessed | tf_op | source)
XLA Modules:
  0.0 147.1 jit_solution(17338135525879982314)
XLA Ops:
  0.6 0.1 pad.2.clone
  0.7 0.7 multiply_bitcast_fusion
  1.4 0.8 slice_bitcast_fusion.3
  2.2 0.6 reduce-window.6
  2.8 0.2 slice_reduce_fusion
  3.0 0.1 fusion
  3.1 0.7 fusion.3
  3.8 0.7 maximum_maximum_fusion.info_ref
  4.5 1.3 bitcast_convert_fusion.gain_ref
  5.8 135.6 %shard_map.121 = (bf16[172,4096]{1,0:T(8,128)(2,1)}, bf16[172,4096]{1,0:T(8,128)(2,1)}, bf16[172,4096]{1,0:T(8,128)(2,1)}) custom-call(bf16[512,1024]{1,0:T(8,128)(2,1)} %bitcast.44, bf16[128,512]{1,0:T(8,128)(2,1)} %context_ref.1, bf16[128,4096]{1,0:T(8,128)(2,1)} %residual_ref.1, bf16[128,4096]{1,0:T(8,128)(2,1)} %cot_ref.1, ...), custom_call_target="tpu_custom_call" | custom-call | tf_op jit(solution)/shard_map/pallas_call | solution.py:525
  141.4 0.0 copy-start.1
  141.4 2.7 %copy.16 = bf16[1,4096,172]{1,2,0:T(8,128)(2,1)} copy(bf16[1,4096,172]{1,2,0:T(8,128)(2,1)} %bitcast.43) | data formatting | bytes 2818048
  144.1 0.0 copy-done.1
  144.1 0.0 copy-start
  144.1 1.1 copy.17
  145.2 0.8 copy-done
  146.0 1.1 copy.18
  (7 shorter events, 0.1 us)
Async XLA Ops:
  141.4 2.7 %copy-start.1 = (bf16[172,4096]{1,0:T(8,128)(2,1)S(1)}, bf16[172,4096]{1,0:T(8,128)(2,1)}, u32[]{:S(2)}) copy-start(bf16[172,4096]{1,0:T(8,128)(2,1)} %get-tuple-element.7) | copy-start | bytes 4227076
  144.1 1.9 %copy-start = (bf16[172,4096]{1,0:T(8,128)(2,1)S(1)}, bf16[172,4096]{1,0:T(8,128)(2,1)}, u32[]{:S(2)}) copy-start(bf16[172,4096]{1,0:T(8,128)(2,1)} %get-tuple-element.8) | copy-start | bytes 4227076

commit v2 on v1

v2 whole, which is shorter than its diff:
```python
import functools

import jax
import jax.numpy as jnp
from jax import lax
from jax.experimental import pallas as pl
from jax.experimental.pallas import tpu as pltpu
from jax.sharding import PartitionSpec as P

MESH = pl.DeviceIdType.MESH
BF = jnp.bfloat16
F32 = jnp.float32
NT = (((1,), (1,)), ((), ()))


class Coords:
    def __init__(self):
        self.z = lax.axis_index("branch")
        self.mp = lax.axis_index("mp")
        self.dp = lax.axis_index("dp")
        self.x = lax.rem(self.mp, 4)
        self.core = lax.rem(self.dp, 2)
        self.y = lax.div(self.dp, 2) * 2 + lax.div(self.mp, 4)

    def at(self, da, db, core):
        other = 1 - core
        x = lax.rem(self.x + other * da + core * db + 8, 4)
        y = lax.rem(self.y + core * da + other * db + 8, 4)
        return x, y

    def device(self, da, db):
        x, y = self.at(da, db, self.core)
        return (self.z, lax.rem(y, 2) * 4 + x, lax.div(y, 2) * 2 + self.core)

    def piece(self, da, db, core=None):
        core = self.core if core is None else core
        x, y = self.at(da, db, core)
        return (lax.div(y, 2) * 2 + core) * 8 + lax.rem(y, 2) * 4 + x

    def sibling(self):
        return (self.z, self.mp, self.dp + 1 - 2 * self.core)


RING = (0, -1, 1, 2)


class PlaneGather:
    COPIES = 36

    def __init__(self, at, buf, send, recv):
        self.at, self.buf, self.send, self.recv = at, buf, send, recv
        self.half = buf.shape[1] // 2
        self.sent = []

    def view(self, piece, half=None):
        if half is None:
            return self.buf.at[piece]
        return self.buf.at[piece, pl.ds(half * self.half, self.half)]

    def copy(self, index, piece, device, half=None):
        ref = self.view(piece, half)
        return pltpu.make_async_remote_copy(
            src_ref=ref,
            dst_ref=ref,
            send_sem=self.send.at[index],
            recv_sem=self.recv.at[index],
            device_id=device,
            device_id_type=MESH,
        )

    def go(self, index, piece, device, half=None):
        descriptor = self.copy(index, piece, device, half)
        descriptor.start()
        self.sent.append(descriptor)

    def arrived(self, index, piece, half=None):
        self.copy(index, piece, self.at.sibling(), half).wait_recv()

    def to_sibling(self, qa, qb):
        index = 20 + 4 * RING.index(qa) + RING.index(qb)
        self.go(index, self.at.piece(qa, qb), self.at.sibling())

    def spread(self, qa):
        index = 4 + 4 * RING.index(qa)
        piece = self.at.piece(qa, 0)
        self.go(index, piece, self.at.device(0, 1))
        self.go(index + 1, piece, self.at.device(0, -1))
        self.to_sibling(qa, 0)

    def start(self):
        piece = self.at.piece(0, 0)
        self.go(0, piece, self.at.device(1, 0))
        self.go(1, piece, self.at.device(-1, 0))
        self.spread(0)

    def first_axis(self):
        low, high = self.at.piece(-1, 0), self.at.piece(1, 0)
        self.arrived(0, low)
        self.go(2, low, self.at.device(1, 0), 0)
        self.arrived(1, high)
        self.go(3, high, self.at.device(-1, 0), 1)
        self.spread(-1)
        self.spread(1)

    def first_axis_far(self):
        far = self.at.piece(2, 0)
        self.arrived(2, far, 0)
        self.arrived(3, far, 1)
        self.spread(2)

    def relay(self, qa):
        index = 4 + 4 * RING.index(qa)
        low, high = self.at.piece(qa, -1), self.at.piece(qa, 1)
        self.arrived(index, low)
        self.go(index + 2, low, self.at.device(0, 1), 0)
        self.arrived(index + 1, high)
        self.go(index + 3, high, self.at.device(0, -1), 1)
        self.to_sibling(qa, -1)
        self.to_sibling(qa, 1)

    def far(self, qa):
        index = 4 + 4 * RING.index(qa)
        piece = self.at.piece(qa, 2)
        self.arrived(index + 2, piece, 0)
        self.arrived(index + 3, piece, 1)
        self.to_sibling(qa, 2)

    def from_sibling(self, qa):
        for qb in RING:
            index = 20 + 4 * RING.index(qa) + RING.index(qb)
            self.arrived(index, self.at.piece(qa, qb, 1 - self.at.core))

    def own_group(self, qa):
        return [self.at.piece(qa, qb) for qb in RING]

    def sibling_group(self, qa):
        return [self.at.piece(qa, qb, 1 - self.at.core) for qb in RING]

    def steps(self):
        return [
            self.start,
            self.first_axis,
            self.first_axis_far,
            functools.partial(self.relay, 0),
            functools.partial(self.relay, -1),
            functools.partial(self.relay, 1),
            functools.partial(self.far, 0),
            functools.partial(self.relay, 2),
            functools.partial(self.far, -1),
            functools.partial(self.far, 1),
            functools.partial(self.far, 2),
        ]

    def finish(self):
        for descriptor in self.sent:
            descriptor.wait_send()


POSITION = {0: 0, 1: 1, 7: 2, 2: 3, 6: 4, 3: 5, 5: 6, 4: 7}
NEAR = 5
SIZE = (NEAR * 160, (8 - NEAR) * 160)
START = (0, SIZE[0])
PARTS = 4
CAP = 40


def kernel(
    attn_ref, context_ref, residual_ref, cot_ref, ids_ref, gates_ref, gain1_ref, wg_ref, wu_ref, wd_ref,
    og_ref, ou_ref, od_ref,
    rows_in0, rows_in1, rows_cot0, rows_cot1, ctx_all, wgu, wd, wtmp, acc0, acc1, back0, back1, ssq0, ssq1, dgu0, dgu1, hid0, hid1,
    part_gu, part_d, stage, gain_ref,
    red_in_l, red_in_s, red_out_l, red_out_s, red_sum, merged_all, attn_acc,
    res_all, cot_all, info_all, sel, route_x, route_c,
    w_sem, in0_send, in0_recv, in1_send, in1_recv, cot0_send, cot0_recv, cot1_send, cot1_recv,
    ctx_send, ctx_recv, in_local, ex_send, ex_recv, ex_local,
    rl_send, rl_recv, rs_send, rs_recv, ma_send, ma_recv, ga_send, ga_recv,
    tx_send, tx_recv, tc_send, tc_recv, out_sem,
):
    at = Coords()
    z, mp, dp = at.z, at.mp, at.dp
    own = at.piece(0, 0)
    hidden = wg_ref.shape[0]
    hid_pad = wgu.shape[0] // 2
    rows_in = (rows_in0, rows_in1)
    acc, acc_back, ssq, dgu, hid = (acc0, acc1), (back0, back1), (ssq0, ssq1), (dgu0, dgu1), (hid0, hid1)
    rows_cot = (rows_cot0, rows_cot1)
    pending = []

    def z_dev(k):
        return (lax.rem(z + k + 8, 8), mp, dp)

    def mp_dev(k):
        return (z, lax.rem(mp + k, 8), dp)

    def dp_dev(k):
        return (z, mp, lax.rem(dp + k, 4))

    def remote(src, dst, send, recv, device):
        return pltpu.make_async_remote_copy(
            src_ref=src, dst_ref=dst, send_sem=send, recv_sem=recv,
            device_id=device, device_id_type=MESH,
        )

    def push(src, dst, send, recv, device):
        descriptor = remote(src, dst, send, recv, device)
        descriptor.start()
        pending.append(descriptor)

    def landed(dst, recv, send):
        remote(dst, dst, send, recv, at.sibling()).wait_recv()

    barrier = pltpu.get_barrier_semaphore()
    peers = [z_dev(k) for k in range(1, 8)] + [mp_dev(k) for k in range(1, 8)]
    peers += [dp_dev(k) for k in range(1, 4)]
    for dy in (1, -1):
        y = lax.rem(at.y + dy + 4, 4)
        peers.append((z, lax.rem(y, 2) * 4 + at.x, lax.div(y, 2) * 2 + at.core))
    for peer in peers:
        pl.semaphore_signal(barrier, inc=1, device_id=peer, device_id_type=MESH)

    ctx_copy = pltpu.make_async_copy(context_ref, ctx_all.at[own], in_local.at[0])
    ctx_copy.start()
    dp_rows = pl.ds(pl.multiple_of(dp * 128, 128), 128)

    def columns(k):
        d = lax.rem(dp + k, 4)
        return pl.ds(pl.multiple_of(d * 1024 + mp * 128, 128), 128)

    locals_ = [
        pltpu.make_async_copy(residual_ref.at[:, columns(0)], res_all.at[dp_rows], ex_local.at[0]),
        pltpu.make_async_copy(cot_ref.at[:, columns(0)], cot_all.at[dp_rows], ex_local.at[1]),
    ]
    for copy in locals_:
        copy.start()

    gain_ref[...] = gain1_ref[...].astype(F32).reshape(32, 128)

    ids = ids_ref[...]
    experts = lax.broadcasted_iota(jnp.int32, (8, 128), 0)
    first = jnp.where(experts == ids[0:1, :], 1.0, 0.0)
    second = jnp.where(experts == ids[1:2, :], 1.0, 0.0)
    before = jnp.where(
        lax.broadcasted_iota(jnp.int32, (128, 128), 0) < lax.broadcasted_iota(jnp.int32, (128, 128), 1),
        1.0, 0.0,
    ).astype(BF)
    counts = jnp.dot(
        jnp.concatenate([first, second], axis=0).astype(BF), before, preferred_element_type=F32
    )
    slot0 = jnp.sum(first * counts[0:8], axis=0, keepdims=True)
    slot1 = jnp.sum(
        second * (counts[8:16] + jnp.sum(first, axis=1, keepdims=True)), axis=0, keepdims=True
    )
    base = (ids * 160 + dp * CAP).astype(F32)
    code0 = jnp.where(slot0 < CAP, base[0:1] + slot0, -1.0)
    code1 = jnp.where(slot1 < CAP, base[1:2] + slot1, -1.0)
    gates = gates_ref[...].astype(F32) / 32768.0
    info_all[dp] = jnp.concatenate([code0, code1, gates, jnp.zeros((4, 128), F32)], axis=0)
    pl.semaphore_wait(barrier, len(peers))

    for k in range(1, 4):
        push(cot_ref.at[:, columns(k)], cot_all.at[dp_rows], ex_send.at[0, k], ex_recv.at[0, k], dp_dev(k))
        push(info_all.at[dp], info_all.at[dp], ex_send.at[1, k], ex_recv.at[1, k], dp_dev(k))

    def chunk(k):
        t = lax.rem(z + k + 8, 8)
        return pl.ds(pl.multiple_of(t * 64, 64), 64)

    width = 1024 // PARTS
    part_cols = [pl.ds(h * width, width) for h in range(PARTS)]

    def reduce_step(step):
        for h in range(PARTS):
            cols = part_cols[h]
            sign = 1 - 2 * (h % 2)
            if step < 4:
                part = chunk(sign * (4 - step))
                src = attn_ref.at[part, cols]
                if step > 0:
                    landed(red_in_l.at[step - 1, h], rl_recv.at[step - 1, h], rl_send.at[step - 1, h])
                    red_out_l[step - 1, h] = (
                        red_in_l[step - 1, h].astype(F32) + attn_ref[part, cols].astype(F32)
                    ).astype(BF)
                    src = red_out_l.at[step - 1, h]
                push(src, red_in_l.at[step, h], rl_send.at[step, h], rl_recv.at[step, h], z_dev(sign))
            if step < 3:
                part = chunk(-sign * (3 - step))
                src = attn_ref.at[part, cols]
                if step > 0:
                    landed(red_in_s.at[step - 1, h], rs_recv.at[step - 1, h], rs_send.at[step - 1, h])
                    red_out_s[step - 1, h] = (
                        red_in_s[step - 1, h].astype(F32) + attn_ref[part, cols].astype(F32)
                    ).astype(BF)
                    src = red_out_s.at[step - 1, h]
                push(src, red_in_s.at[step, h], rs_send.at[step, h], rs_recv.at[step, h], z_dev(-sign))

    reduce_step(0)

    ctx_gather = PlaneGather(at, ctx_all, ctx_send, ctx_recv)
    cot_gather = (
        PlaneGather(at, rows_cot0, cot0_send, cot0_recv), PlaneGather(at, rows_cot1, cot1_send, cot1_recv)
    )
    in_gather = (
        PlaneGather(at, rows_in0, in0_send, in0_recv), PlaneGather(at, rows_in1, in1_send, in1_recv)
    )
    ctx_steps = ctx_gather.steps()
    cot_steps = [gather.steps() for gather in cot_gather]
    in_steps = [gather.steps() for gather in in_gather]

    def run(steps, count=1):
        for _ in range(count):
            if steps:
                steps.pop(0)()

    ctx_copy.wait()
    run(ctx_steps)

    weights = [
        pltpu.make_async_copy(wg_ref, wtmp.at[0], w_sem.at[0]),
        pltpu.make_async_copy(wu_ref, wtmp.at[1], w_sem.at[1]),
        pltpu.make_async_copy(wd_ref, wd, w_sem.at[2]),
    ]
    for copy in weights:
        copy.start()

    def from_group(k):
        d = lax.rem(dp - k + 4, 4)
        return pl.ds(pl.multiple_of(d * 128, 128), 128), d

    reduce_step(1)
    locals_[1].wait()
    for k in range(1, 4):
        rows, d = from_group(k)
        landed(cot_all.at[rows], ex_recv.at[0, k], ex_send.at[0, k])
        landed(info_all.at[d], ex_recv.at[1, k], ex_send.at[1, k])

    @pl.loop(0, 8)
    def _(e):
        place = (lax.broadcasted_iota(jnp.int32, (160, 128), 0) + e * 160).astype(F32)
        row_gate = jnp.zeros((160, 1), F32)
        rows = pl.ds(pl.multiple_of(e * 160, 160), 160)
        for d in range(4):
            info = info_all[d]
            first = place == info[0:1, :]
            second = place == info[1:2, :]
            sel[rows, d * 128:(d + 1) * 128] = jnp.where(first | second, 1.0, 0.0).astype(BF)
            gates = jnp.where(first, info[2:3, :], jnp.where(second, info[3:4, :], 0.0))
            row_gate += jnp.sum(gates, axis=1, keepdims=True)
        picked = jnp.dot(sel[rows, :], cot_all[...], preferred_element_type=F32)
        route_c[e] = (picked * row_gate).astype(BF)

    def block(k):
        place = POSITION[k]
        if place < NEAR:
            return 0, pl.ds(place * 160, 160)
        return 1, pl.ds((place - NEAR) * 160, 160)

    def exchange(route, gathered, send, recv, wanted):
        for k in sorted(range(1, 8), key=lambda k: POSITION[k]):
            half, rows = block(k)
            e = lax.rem(z - k + 8, 8)
            if half == wanted:
                push(route.at[e], gathered[half].at[own, rows], send.at[k], recv.at[k], z_dev(-k))
        if wanted == 0:
            half, rows = block(0)
            gathered[half][own, rows, :] = route[z]

    def exchanged(gathered, send, recv, wanted):
        for k in range(1, 8):
            half, rows = block(k)
            if half == wanted:
                landed(gathered[half].at[own, rows], recv.at[k], send.at[k])

    exchange(route_c, rows_cot, tc_send, tc_recv, 0)

    run(ctx_steps)
    reduce_step(2)
    for k in range(1, 4):
        push(residual_ref.at[:, columns(k)], res_all.at[dp_rows], ex_send.at[2, k], ex_recv.at[2, k], dp_dev(k))
    run(ctx_steps, 4)
    reduce_step(3)
    exchanged(rows_cot, tc_send, tc_recv, 0)
    run(cot_steps[0])
    run(ctx_steps, 3)

    for h in range(PARTS):
        landed(red_in_l.at[3, h], rl_recv.at[3, h], rl_send.at[3, h])
        landed(red_in_s.at[2, h], rs_recv.at[2, h], rs_send.at[2, h])
        total = (
            red_in_l[3, h].astype(F32) + red_in_s[2, h].astype(F32)
            + attn_ref[chunk(0), part_cols[h]].astype(F32)
        )
        mean = (total * 0.125).astype(BF)
        for part in range(8 // PARTS):
            red_sum[8 // PARTS * h + part] = mean[:, part * 128:(part + 1) * 128]
    exchange(route_c, rows_cot, tc_send, tc_recv, 1)
    own_rows = pl.ds(pl.multiple_of(z * 64, 64), 64)
    for k in range(1, 8):
        j = lax.rem(mp + k, 8)
        push(red_sum.at[j], merged_all.at[mp, own_rows], ma_send.at[k], ma_recv.at[k], mp_dev(k))
    merged_all[mp, own_rows, :] = red_sum[mp]
    run(cot_steps[0])
    for k in range(1, 8):
        j = lax.rem(mp - k + 8, 8)
        landed(merged_all.at[j, own_rows], ma_recv.at[k], ma_send.at[k])

    def merged_view(k, h):
        t = lax.rem(z + k + 8, 8)
        return merged_all.at[pl.ds(8 // PARTS * h, 8 // PARTS), pl.ds(pl.multiple_of(t * 64, 64), 64)]

    def gather_step(step):
        for h in range(PARTS):
            sign = 1 - 2 * (h % 2)
            if step > 0:
                landed(merged_view(-sign * step, h), ga_recv.at[0, step - 1, h], ga_send.at[0, step - 1, h])
            if step < 4:
                view = merged_view(-sign * step, h)
                push(view, view, ga_send.at[0, step, h], ga_recv.at[0, step, h], z_dev(sign))
            if 0 < step < 4:
                landed(merged_view(sign * step, h), ga_recv.at[1, step - 1, h], ga_send.at[1, step - 1, h])
            if step < 3:
                view = merged_view(sign * step, h)
                push(view, view, ga_send.at[1, step, h], ga_recv.at[1, step, h], z_dev(-sign))

    gather_step(0)
    run(ctx_steps, 2)
    run(cot_steps[0], 2)
    exchanged(rows_cot, tc_send, tc_recv, 1)
    run(cot_steps[1])
    gather_step(1)
    run(cot_steps[0], 2)
    gather_step(2)
    run(cot_steps[1])
    run(cot_steps[0])
    gather_step(3)
    run(cot_steps[0], 2)
    run(cot_steps[1])
    gather_step(4)
    for qa in RING:
        ctx_gather.from_sibling(qa)
    for k in range(1, 4):
        rows, _ = from_group(k)
        landed(res_all.at[rows], ex_recv.at[2, k], ex_send.at[2, k])
    locals_[0].wait()

    def lanes(piece):
        return pl.ds(pl.multiple_of(piece * 128, 128), 128)

    def gain_of(piece):
        return gain_ref[pl.ds(piece, 1), :]

    for j in range(8):
        context = jnp.concatenate([ctx_all[d * 8 + j] for d in range(4)], axis=0)
        product = jnp.dot(context, merged_all[j], preferred_element_type=F32)
        if j == 0:
            attn_acc[...] = product + res_all[...].astype(F32)
        else:
            attn_acc[...] += product
    res_all[...] = (attn_acc[...] * gain_of(own)).astype(BF)

    @pl.loop(0, 8)
    def _(e):
        rows = pl.ds(pl.multiple_of(e * 160, 160), 160)
        route_x[e] = jnp.dot(sel[rows, :], res_all[...], preferred_element_type=F32).astype(BF)

    exchange(route_x, rows_in, tx_send, tx_recv, 0)

    for copy in weights:
        copy.wait()
    wgu[0:hidden, :] = wtmp[0]
    wgu[hid_pad:hid_pad + hidden, :] = wtmp[1]
    for ref in acc + acc_back + ssq:
        ref[...] = jnp.zeros_like(ref)

    def tiles(half):
        return [(start, min(256, SIZE[half] - start)) for start in range(0, SIZE[half], 256)]

    def back_group(half, group):
        lhs = jnp.concatenate([wd[:, lanes(p)] for p in group], axis=1)
        for start, width in tiles(half):
            rhs = jnp.concatenate([rows_cot[half][p, start:start + width, :] for p in group], axis=1)
            cols = slice(start, start + width)
            acc_back[half][:, cols] += lax.dot_general(lhs, rhs, NT, preferred_element_type=F32)

    def fore_group(half, group):
        lhs = jnp.concatenate([wgu[:, lanes(p)] for p in group], axis=1)
        inverse = [1.0 / gain_of(p) for p in group]
        for start, width in tiles(half):
            parts = [rows_in[half][p, start:start + width, :] for p in group]
            cols = slice(start, start + width)
            acc[half][:, cols] += lax.dot_general(
                lhs, jnp.concatenate(parts, axis=1), NT, preferred_element_type=F32
            )
            squares = ssq[half][cols, :]
            for part, scale in zip(parts, inverse):
                value = part.astype(F32) * scale
                squares += value * value
            ssq[half][cols, :] = squares

    def own_back(half, *places):
        for qa in places:
            back_group(half, cot_gather[half].own_group(qa))

    def sibling_back(half, *places):
        for qa in places:
            cot_gather[half].from_sibling(qa)
            back_group(half, cot_gather[half].sibling_group(qa))

    def own_fore(half, *places):
        for qa in places:
            fore_group(half, in_gather[half].own_group(qa))

    def sibling_fore(half, *places):
        for qa in places:
            in_gather[half].from_sibling(qa)
            fore_group(half, in_gather[half].sibling_group(qa))

    def activations(half):
        for start in range(0, SIZE[half], 128):
            cols = slice(start, min(start + 128, SIZE[half]))
            squares = lax.dot_general(
                jnp.ones((8, 128), BF), ssq[half][cols, :].astype(BF), NT, preferred_element_type=F32
            )
            inv = lax.rsqrt(squares[0:1] * (1.0 / 4096.0) + 1e-05)
            gate = acc[half][0:hidden, cols] * inv
            up = acc[half][hid_pad:hid_pad + hidden, cols] * inv
            back = acc_back[half][:, cols]
            sig = jax.nn.sigmoid(gate)
            active = gate * sig
            hid[half][:, cols] = (active * up).astype(BF)
            back = back * inv
            dgu[half][0:hidden, cols] = (back * up * sig * (1.0 + gate * (1.0 - sig))).astype(BF)
            dgu[half][hid_pad:hid_pad + hidden, cols] = (back * active).astype(BF)

    def gradients(half, chunk):
        @pl.loop(0, 4)
        def _(i):
            n = chunk * 4 + i
            cols = pl.ds(pl.multiple_of(n * 256, 256), 256)
            rhs = jnp.concatenate([rows_in[half][2 * n], rows_in[half][2 * n + 1]], axis=1)
            both = jnp.dot(dgu[half][...], rhs, preferred_element_type=F32)
            rhs = jnp.concatenate([rows_cot[half][2 * n], rows_cot[half][2 * n + 1]], axis=1)
            down = jnp.dot(hid[half][...], rhs, preferred_element_type=F32)
            if half == 0:
                part_gu[:, cols] = both
                part_d[:, cols] = down
            else:
                both = (both + part_gu[:, cols]).astype(BF)
                stage[0, :, cols] = both[0:hidden]
                stage[1, :, cols] = both[hid_pad:hid_pad + hidden]
                stage[2, :, cols] = (down + part_d[:, cols]).astype(BF)

    run(cot_steps[1], 2)
    run(cot_steps[0], 3)
    run(cot_steps[1], 1)
    exchanged(rows_in, tx_send, tx_recv, 0)
    exchange(route_x, rows_in, tx_send, tx_recv, 1)
    run(in_steps[0])
    run(cot_steps[1], 2)
    own_back(0, 0, -1, 1, 2)
    run(cot_steps[1], 2)
    run(in_steps[0])
    run(cot_steps[1], 1)
    sibling_back(0, 0, -1)
    run(in_steps[0])
    sibling_back(0, 1, 2)
    run(in_steps[0], 3)
    own_back(1, 0, -1, 1, 2)
    exchanged(rows_in, tx_send, tx_recv, 1)
    run(in_steps[1])
    sibling_back(1, 0, -1, 1, 2)
    run(in_steps[0], 2)
    own_fore(0, 0)
    run(in_steps[1])
    run(in_steps[0])
    own_fore(0, -1)
    run(in_steps[0])
    own_fore(0, 1)
    run(in_steps[1])
    sibling_fore(0, 0)
    run(in_steps[0])
    own_fore(0, 2)
    run(in_steps[1])
    sibling_fore(0, -1, 1)
    run(in_steps[1], 2)
    sibling_fore(0, 2)
    run(in_steps[1], 2)
    activations(0)
    gradients(0, 0)
    run(in_steps[1])
    gradients(0, 1)
    run(in_steps[1])
    gradients(0, 2)
    run(in_steps[1])
    gradients(0, 3)
    while in_steps[1]:
        run(in_steps[1])
    own_fore(1, 0, -1, 1, 2)
    sibling_fore(1, 0, -1, 1, 2)
    activations(1)
    outs = (og_ref, ou_ref, od_ref)
    writes = []
    for quarter in range(4):
        gradients(1, quarter)
        cols = pl.ds(quarter * 1024, 1024)
        for index in range(3):
            write = pltpu.make_async_copy(
                stage.at[index, :, cols], outs[index].at[:, cols], out_sem.at[index, quarter]
            )
            write.start()
            writes.append(write)

    assert not any([ctx_steps] + cot_steps + in_steps)
    for gather in (ctx_gather,) + cot_gather + in_gather:
        gather.finish()
    for descriptor in pending:
        descriptor.wait_send()
    for write in writes:
        write.wait()


def write_kernel(*refs):
    count = 3
    sources, outs, hold, sem_in, sem_out = refs[:count], refs[count:2 * count], *refs[2 * count:]
    reads, writes = [], []
    for index in range(count):
        for part in range(4):
            cols = pl.ds(part * 1024, 1024)
            there = hold.at[index, :, cols]
            reads.append(pltpu.make_async_copy(sources[index].at[:, cols], there, sem_in.at[index, part]))
            writes.append(pltpu.make_async_copy(there, outs[index].at[:, cols], sem_out.at[index, part]))
    for read in reads:
        read.start()
    for read, write in zip(reads, writes):
        read.wait()
        write.start()
    for write in writes:
        write.wait()


def per_device(
    context, residual, attn_weight, norm_gain, gate_weight, up_weight, down_weight,
    cotangent, expert_ids, gate_fixed,
):
    hidden = gate_weight.shape[2]
    pad = 176
    dma = pltpu.SemaphoreType.DMA
    vmem = pl.BlockSpec(memory_space=pltpu.VMEM)
    hbm = pl.BlockSpec(memory_space=pl.ANY)
    out = jax.ShapeDtypeStruct((hidden, 4096), BF)
    copies = PlaneGather.COPIES
    near, far = SIZE
    grads = pl.pallas_call(
        kernel,
        out_shape=(out, out, out),
        in_specs=[vmem, hbm, hbm, hbm, vmem, vmem, vmem, hbm, hbm, hbm],
        out_specs=(hbm, hbm, hbm),
        scratch_shapes=[
            pltpu.VMEM((32, near, 128), BF),
            pltpu.VMEM((32, far, 128), BF),
            pltpu.VMEM((32, near, 128), BF),
            pltpu.VMEM((32, far, 128), BF),
            pltpu.VMEM((32, 128, 512), BF),
            pltpu.VMEM((2 * pad, 4096), BF),
            pltpu.VMEM((hidden, 4096), BF),
            pltpu.VMEM((2, hidden, 4096), BF),
            pltpu.VMEM((2 * pad, near), F32),
            pltpu.VMEM((2 * pad, far), F32),
            pltpu.VMEM((hidden, near), F32),
            pltpu.VMEM((hidden, far), F32),
            pltpu.VMEM((near, 128), F32),
            pltpu.VMEM((far, 128), F32),
            pltpu.VMEM((2 * pad, near), BF),
            pltpu.VMEM((2 * pad, far), BF),
            pltpu.VMEM((hidden, near), BF),
            pltpu.VMEM((hidden, far), BF),
            pltpu.VMEM((2 * pad, 4096), F32),
            pltpu.VMEM((hidden, 4096), F32),
            pltpu.VMEM((3, hidden, 4096), BF),
            pltpu.VMEM((32, 128), F32),
            pltpu.VMEM((4, PARTS, 64, 1024 // PARTS), BF),
            pltpu.VMEM((3, PARTS, 64, 1024 // PARTS), BF),
            pltpu.VMEM((3, PARTS, 64, 1024 // PARTS), BF),
            pltpu.VMEM((2, PARTS, 64, 1024 // PARTS), BF),
            pltpu.VMEM((8, 64, 128), BF),
            pltpu.VMEM((8, 512, 128), BF),
            pltpu.VMEM((512, 128), F32),
            pltpu.VMEM((512, 128), BF),
            pltpu.VMEM((512, 128), BF),
            pltpu.VMEM((4, 8, 128), F32),
            pltpu.VMEM((1280, 512), BF),
            pltpu.VMEM((8, 160, 128), BF),
            pltpu.VMEM((8, 160, 128), BF),
            dma((3,)),
            dma((copies,)), dma((copies,)), dma((copies,)), dma((copies,)),
            dma((copies,)), dma((copies,)), dma((copies,)), dma((copies,)),
            dma((copies,)), dma((copies,)), dma((1,)),
            dma((3, 4)), dma((3, 4)), dma((2,)),
            dma((4, PARTS)), dma((4, PARTS)), dma((3, PARTS)), dma((3, PARTS)),
            dma((8,)), dma((8,)),
            dma((2, 4, PARTS)), dma((2, 4, PARTS)),
            dma((8,)), dma((8,)),
            dma((8,)), dma((8,)),
            dma((3, 4)),
        ],
        compiler_params=pltpu.CompilerParams(
            collective_id=0, has_side_effects=True, vmem_limit_bytes=67_000_000
        ),
    )(
        attn_weight[0], context, residual, cotangent, expert_ids.T, gate_fixed.T, norm_gain,
        gate_weight[0].T, up_weight[0].T, down_weight[0],
    )
    grads = pl.pallas_call(
        write_kernel,
        out_shape=(out, out, out),
        in_specs=[hbm, hbm, hbm],
        out_specs=(hbm, hbm, hbm),
        scratch_shapes=[pltpu.VMEM((3, hidden, 4096), BF), dma((3, 4)), dma((3, 4))],
    )(*grads)
    return grads[0].T[None], grads[1].T[None], grads[2][None]


def solution(mesh):
    return jax.shard_map(
        per_device,
        mesh=mesh,
        in_specs=(
            P(("branch", "dp"), "mp"),
            P(("branch", "dp"), None),
            P("branch", "mp", "dp"),
            P(),
            P("branch", None, ("mp", "dp")),
            P("branch", None, ("mp", "dp")),
            P("branch", ("mp", "dp"), None),
            P(("branch", "dp"), None),
            P(("branch", "dp"), None),
            P(("branch", "dp"), None),
        ),
        out_specs=(
            P("branch", None, ("mp", "dp")),
            P("branch", None, ("mp", "dp")),
            P("branch", ("mp", "dp"), None),
        ),
        check_vma=False,
    )
```

time: 147 us -> 118 us (0.80)
  the two profiles are of different devices: /device:TPU:9 before, /device:TPU:32 now
where the time goes in v2:
time: 118 us; the launch traced here: 117 us
  Pallas kernels  116 us (98%)
    pallas_call x1, Pallas kernels, per_device(): pl.pallas_call(kernel, out_shape=(out, out, out), in_specs=[vmem, hbm, hb...  112 us
    pallas_call x1, Pallas kernels, per_device(): pl.pallas_call(write_kernel, out_shape=(out, out, out), in_specs=[hbm, hb...  3.92 us

profile of v2, /device:TPU:32, one launch (start us, length us, event | category | flops | bytes accessed | tf_op | source)
XLA Modules:
  0.0 116.7 jit_solution(8830277903476207722)
XLA Ops:
  0.6 112.0 %shard_map.121 = (bf16[172,4096]{1,0:T(8,128)(2,1)}, bf16[172,4096]{1,0:T(8,128)(2,1)}, bf16[172,4096]{1,0:T(8,128)(2,1)}) custom-call(bf16[512,1024]{1,0:T(8,128)(2,1)} %bitcast.20, bf16[128,512]{1,0:T(8,128)(2,1)} %context_ref.1, bf16[128,4096]{1,0:T(8,128)(2,1)} %residual_ref.1, bf16[128,4096]{1,0:T(8,128)(2,1)} %cot_ref.1, s32[2,128]{1,0:T(2,128)} %bitcast.21, ...), custom_call_target="tpu_custom_call" | custom-call | tf_op jit(solution)/shard_map/pallas_call | solution.py:652
  112.7 3.9 %shard_map.122 = (bf16[172,4096]{1,0:T(8,128)(2,1)}, bf16[172,4096]{1,0:T(8,128)(2,1)}, bf16[172,4096]{1,0:T(8,128)(2,1)}) custom-call(bf16[172,4096]{1,0:T(8,128)(2,1)} %get-tuple-element.9.refs_0_, bf16[172,4096]{1,0:T(8,128)(2,1)} %get-tuple-element.10.refs_1_, bf16[172,4096]{1,0:T(8,128)(2,1)} %get-tuple-element.11.refs_2_), custom_call_target="tpu_custom_call" | custom-call | tf_op jit(solution)/shard_map/pallas_call | solution.py:712

commit v3 on v2

--- a/solution.py
+++ b/solution.py
@@ -47,15 +47,16 @@
 class PlaneGather:
     COPIES = 36
 
-    def __init__(self, at, buf, send, recv):
+    def __init__(self, at, buf, send, recv, start=0, size=None):
         self.at, self.buf, self.send, self.recv = at, buf, send, recv
-        self.half = buf.shape[1] // 2
+        self.base, self.size = start, buf.shape[1] if size is None else size
+        self.half = self.size // 2
         self.sent = []
 
     def view(self, piece, half=None):
         if half is None:
-            return self.buf.at[piece]
-        return self.buf.at[piece, pl.ds(half * self.half, self.half)]
+            return self.buf.at[piece, pl.ds(self.base, self.size)]
+        return self.buf.at[piece, pl.ds(self.base + half * self.half, self.half)]
 
     def copy(self, index, piece, device, half=None):
         ref = self.view(piece, half)
@@ -144,8 +145,8 @@
             functools.partial(self.relay, 0),
             functools.partial(self.relay, -1),
             functools.partial(self.relay, 1),
+            functools.partial(self.relay, 2),
             functools.partial(self.far, 0),
-            functools.partial(self.relay, 2),
             functools.partial(self.far, -1),
             functools.partial(self.far, 1),
             functools.partial(self.far, 2),
@@ -159,19 +160,21 @@
 POSITION = {0: 0, 1: 1, 7: 2, 2: 3, 6: 4, 3: 5, 5: 6, 4: 7}
 NEAR = 5
 SIZE = (NEAR * 160, (8 - NEAR) * 160)
-START = (0, SIZE[0])
+WHOLE = SIZE[0] // 256 * 256
+LEFT = SIZE[0] - WHOLE
 PARTS = 4
 CAP = 40
 
 
 def kernel(
-    attn_ref, context_ref, residual_ref, cot_ref, ids_ref, gates_ref, gain1_ref, wg_ref, wu_ref, wd_ref,
+    attn_hbm, context_ref, residual_ref, cot_ref, ids_ref, gates_ref, gain1_ref, wg_ref, wu_ref, wd_ref,
     og_ref, ou_ref, od_ref,
     rows_in0, rows_in1, rows_cot0, rows_cot1, ctx_all, wgu, wd, wtmp, acc0, acc1, back0, back1, ssq0, ssq1, dgu0, dgu1, hid0, hid1,
-    part_gu, part_d, stage, gain_ref,
+    part_gu, part_d, stage, gain_ref, attn_ref,
     red_in_l, red_in_s, red_out_l, red_out_s, red_sum, merged_all, attn_acc,
     res_all, cot_all, info_all, sel, route_x, route_c,
-    w_sem, in0_send, in0_recv, in1_send, in1_recv, cot0_send, cot0_recv, cot1_send, cot1_recv,
+    w_sem, in0_send, in0_recv, in1_send, in1_recv,
+    cotz_send, cotz_recv, cot0_send, cot0_recv, cot1_send, cot1_recv,
     ctx_send, ctx_recv, in_local, ex_send, ex_recv, ex_local,
     rl_send, rl_recv, rs_send, rs_recv, ma_send, ma_recv, ga_send, ga_recv,
     tx_send, tx_recv, tc_send, tc_recv, out_sem,
@@ -230,6 +233,8 @@
         pltpu.make_async_copy(residual_ref.at[:, columns(0)], res_all.at[dp_rows], ex_local.at[0]),
         pltpu.make_async_copy(cot_ref.at[:, columns(0)], cot_all.at[dp_rows], ex_local.at[1]),
     ]
+    attn_copy = pltpu.make_async_copy(attn_hbm, attn_ref, in_local.at[1])
+    attn_copy.start()
     for copy in locals_:
         copy.start()
 
@@ -274,7 +279,7 @@
             sign = 1 - 2 * (h % 2)
             if step < 4:
                 part = chunk(sign * (4 - step))
-                src = attn_ref.at[part, cols]
+                src = attn_hbm.at[part, cols]
                 if step > 0:
                     landed(red_in_l.at[step - 1, h], rl_recv.at[step - 1, h], rl_send.at[step - 1, h])
                     red_out_l[step - 1, h] = (
@@ -284,7 +289,7 @@
                 push(src, red_in_l.at[step, h], rl_send.at[step, h], rl_recv.at[step, h], z_dev(sign))
             if step < 3:
                 part = chunk(-sign * (3 - step))
-                src = attn_ref.at[part, cols]
+                src = attn_hbm.at[part, cols]
                 if step > 0:
                     landed(red_in_s.at[step - 1, h], rs_recv.at[step - 1, h], rs_send.at[step - 1, h])
                     red_out_s[step - 1, h] = (
@@ -296,11 +301,15 @@
     reduce_step(0)
 
     ctx_gather = PlaneGather(at, ctx_all, ctx_send, ctx_recv)
+    rest = SIZE[0] - 160
     cot_gather = (
-        PlaneGather(at, rows_cot0, cot0_send, cot0_recv), PlaneGather(at, rows_cot1, cot1_send, cot1_recv)
+        PlaneGather(at, rows_cot0, cot0_send, cot0_recv, 160, rest),
+        PlaneGather(at, rows_cot1, cot1_send, cot1_recv),
+        PlaneGather(at, rows_cot0, cotz_send, cotz_recv, 0, 160),
     )
     in_gather = (
-        PlaneGather(at, rows_in0, in0_send, in0_recv), PlaneGather(at, rows_in1, in1_send, in1_recv)
+        PlaneGather(at, rows_in0, in0_send, in0_recv),
+        PlaneGather(at, rows_in1, in1_send, in1_recv),
     )
     ctx_steps = ctx_gather.steps()
     cot_steps = [gather.steps() for gather in cot_gather]
@@ -326,6 +335,7 @@
         d = lax.rem(dp - k + 4, 4)
         return pl.ds(pl.multiple_of(d * 128, 128), 128), d
 
+    attn_copy.wait()
     reduce_step(1)
     locals_[1].wait()
     for k in range(1, 4):
@@ -355,14 +365,14 @@
         return 1, pl.ds((place - NEAR) * 160, 160)
 
     def exchange(route, gathered, send, recv, wanted):
+        if wanted == 0:
+            half, rows = block(0)
+            gathered[half][own, rows, :] = route[z]
         for k in sorted(range(1, 8), key=lambda k: POSITION[k]):
             half, rows = block(k)
             e = lax.rem(z - k + 8, 8)
             if half == wanted:
                 push(route.at[e], gathered[half].at[own, rows], send.at[k], recv.at[k], z_dev(-k))
-        if wanted == 0:
-            half, rows = block(0)
-            gathered[half][own, rows, :] = route[z]
 
     def exchanged(gathered, send, recv, wanted):
         for k in range(1, 8):
@@ -370,17 +380,18 @@
             if half == wanted:
                 landed(gathered[half].at[own, rows], recv.at[k], send.at[k])
 
-    exchange(route_c, rows_cot, tc_send, tc_recv, 0)
-
+    cot_near, cot_far, cot_own = cot_steps
+    in_near, in_far = in_steps
     run(ctx_steps)
     reduce_step(2)
+    exchange(route_c, rows_cot, tc_send, tc_recv, 0)
+    run(cot_own)
     for k in range(1, 4):
         push(residual_ref.at[:, columns(k)], res_all.at[dp_rows], ex_send.at[2, k], ex_recv.at[2, k], dp_dev(k))
-    run(ctx_steps, 4)
+    run(ctx_steps, 2)
     reduce_step(3)
-    exchanged(rows_cot, tc_send, tc_recv, 0)
-    run(cot_steps[0])
-    run(ctx_steps, 3)
+    run(cot_own)
+    run(ctx_steps, 2)
 
     for h in range(PARTS):
         landed(red_in_l.at[3, h], rl_recv.at[3, h], rl_send.at[3, h])
@@ -392,13 +403,16 @@
         mean = (total * 0.125).astype(BF)
         for part in range(8 // PARTS):
             red_sum[8 // PARTS * h + part] = mean[:, part * 128:(part + 1) * 128]
-    exchange(route_c, rows_cot, tc_send, tc_recv, 1)
     own_rows = pl.ds(pl.multiple_of(z * 64, 64), 64)
     for k in range(1, 8):
         j = lax.rem(mp + k, 8)
         push(red_sum.at[j], merged_all.at[mp, own_rows], ma_send.at[k], ma_recv.at[k], mp_dev(k))
     merged_all[mp, own_rows, :] = red_sum[mp]
-    run(cot_steps[0])
+    exchange(route_c, rows_cot, tc_send, tc_recv, 1)
+    exchanged(rows_cot, tc_send, tc_recv, 0)
+    run(cot_near)
+    run(ctx_steps)
+    run(cot_own, 2)
     for k in range(1, 8):
         j = lax.rem(mp - k + 8, 8)
         landed(merged_all.at[j, own_rows], ma_recv.at[k], ma_send.at[k])
@@ -423,17 +437,19 @@
 
     gather_step(0)
     run(ctx_steps, 2)
-    run(cot_steps[0], 2)
+    run(cot_own, 2)
+    run(cot_near)
+    gather_step(1)
+    run(cot_near, 2)
     exchanged(rows_cot, tc_send, tc_recv, 1)
-    run(cot_steps[1])
-    gather_step(1)
-    run(cot_steps[0], 2)
+    run(cot_far)
+    run(ctx_steps, 2)
     gather_step(2)
-    run(cot_steps[1])
-    run(cot_steps[0])
+    run(cot_near, 2)
+    run(cot_own)
     gather_step(3)
-    run(cot_steps[0], 2)
-    run(cot_steps[1])
+    run(cot_far)
+    run(cot_near)
     gather_step(4)
     for qa in RING:
         ctx_gather.from_sibling(qa)
@@ -502,6 +518,8 @@
 
     def sibling_back(half, *places):
         for qa in places:
+            if half == 0:
+                cot_gather[2].from_sibling(qa)
             cot_gather[half].from_sibling(qa)
             back_group(half, cot_gather[half].sibling_group(qa))
 
@@ -517,6 +535,9 @@
     def activations(half):
         for start in range(0, SIZE[half], 128):
             cols = slice(start, min(start + 128, SIZE[half]))
+            into, place = half, cols
+            if half == 0 and start >= WHOLE:
+                into, place = 1, slice(SIZE[1] + start - WHOLE, SIZE[1] + cols.stop - WHOLE)
             squares = lax.dot_general(
                 jnp.ones((8, 128), BF), ssq[half][cols, :].astype(BF), NT, preferred_element_type=F32
             )
@@ -526,20 +547,28 @@
             back = acc_back[half][:, cols]
             sig = jax.nn.sigmoid(gate)
             active = gate * sig
-            hid[half][:, cols] = (active * up).astype(BF)
+            hid[into][:, place] = (active * up).astype(BF)
             back = back * inv
-            dgu[half][0:hidden, cols] = (back * up * sig * (1.0 + gate * (1.0 - sig))).astype(BF)
-            dgu[half][hid_pad:hid_pad + hidden, cols] = (back * active).astype(BF)
+            dgu[into][0:hidden, place] = (back * up * sig * (1.0 + gate * (1.0 - sig))).astype(BF)
+            dgu[into][hid_pad:hid_pad + hidden, place] = (back * active).astype(BF)
+
+    def contracted(half, parts, n):
+        if half == 0:
+            pair = [parts[0][2 * n + i, 0:WHOLE, :] for i in range(2)]
+        else:
+            pair = [
+                jnp.concatenate([parts[1][2 * n + i], parts[0][2 * n + i, WHOLE:WHOLE + LEFT, :]], axis=0)
+                for i in range(2)
+            ]
+        return jnp.concatenate(pair, axis=1)
 
     def gradients(half, chunk):
-        @pl.loop(0, 4)
+        @pl.loop(0, 4, unroll=2)
         def _(i):
             n = chunk * 4 + i
             cols = pl.ds(pl.multiple_of(n * 256, 256), 256)
-            rhs = jnp.concatenate([rows_in[half][2 * n], rows_in[half][2 * n + 1]], axis=1)
-            both = jnp.dot(dgu[half][...], rhs, preferred_element_type=F32)
-            rhs = jnp.concatenate([rows_cot[half][2 * n], rows_cot[half][2 * n + 1]], axis=1)
-            down = jnp.dot(hid[half][...], rhs, preferred_element_type=F32)
+            both = jnp.dot(dgu[half][...], contracted(half, rows_in, n), preferred_element_type=F32)
+            down = jnp.dot(hid[half][...], contracted(half, rows_cot, n), preferred_element_type=F32)
             if half == 0:
                 part_gu[:, cols] = both
                 part_d[:, cols] = down
@@ -549,51 +578,53 @@
                 stage[1, :, cols] = both[hid_pad:hid_pad + hidden]
                 stage[2, :, cols] = (down + part_d[:, cols]).astype(BF)
 
-    run(cot_steps[1], 2)
-    run(cot_steps[0], 3)
-    run(cot_steps[1], 1)
+    run(cot_far, 3)
+    run(cot_near, 2)
+    run(cot_far)
+    run(cot_near, 2)
+    run(cot_far)
     exchanged(rows_in, tx_send, tx_recv, 0)
+    run(in_near)
+    run(cot_own, 4)
+    run(cot_far, 3)
+    own_back(0, 0, -1, 1, 2)
+    run(in_near)
+    run(cot_far)
     exchange(route_x, rows_in, tx_send, tx_recv, 1)
-    run(in_steps[0])
-    run(cot_steps[1], 2)
-    own_back(0, 0, -1, 1, 2)
-    run(cot_steps[1], 2)
-    run(in_steps[0])
-    run(cot_steps[1], 1)
     sibling_back(0, 0, -1)
-    run(in_steps[0])
+    run(in_near)
     sibling_back(0, 1, 2)
-    run(in_steps[0], 3)
+    run(in_near, 3)
+    exchanged(rows_in, tx_send, tx_recv, 1)
+    run(in_far)
     own_back(1, 0, -1, 1, 2)
-    exchanged(rows_in, tx_send, tx_recv, 1)
-    run(in_steps[1])
+    run(in_near)
     sibling_back(1, 0, -1, 1, 2)
-    run(in_steps[0], 2)
+    run(in_near)
     own_fore(0, 0)
-    run(in_steps[1])
-    run(in_steps[0])
+    run(in_near)
     own_fore(0, -1)
-    run(in_steps[0])
+    run(in_far)
+    run(in_near)
     own_fore(0, 1)
-    run(in_steps[1])
+    run(in_near)
+    run(in_far)
+    own_fore(0, 2)
+    run(in_far)
     sibling_fore(0, 0)
-    run(in_steps[0])
-    own_fore(0, 2)
-    run(in_steps[1])
-    sibling_fore(0, -1, 1)
-    run(in_steps[1], 2)
+    run(in_far)
+    sibling_fore(0, -1)
+    run(in_far, 2)
+    sibling_fore(0, 1)
     sibling_fore(0, 2)
-    run(in_steps[1], 2)
+    run(in_far, 2)
     activations(0)
     gradients(0, 0)
-    run(in_steps[1])
+    run(in_far)
     gradients(0, 1)
-    run(in_steps[1])
+    run(in_far)
     gradients(0, 2)
-    run(in_steps[1])
     gradients(0, 3)
-    while in_steps[1]:
-        run(in_steps[1])
     own_fore(1, 0, -1, 1, 2)
     sibling_fore(1, 0, -1, 1, 2)
     activations(1)
@@ -652,7 +683,7 @@
     grads = pl.pallas_call(
         kernel,
         out_shape=(out, out, out),
-        in_specs=[vmem, hbm, hbm, hbm, vmem, vmem, vmem, hbm, hbm, hbm],
+        in_specs=[hbm, hbm, hbm, hbm, vmem, vmem, vmem, hbm, hbm, hbm],
         out_specs=(hbm, hbm, hbm),
         scratch_shapes=[
             pltpu.VMEM((32, near, 128), BF),
@@ -669,14 +700,15 @@
             pltpu.VMEM((hidden, far), F32),
             pltpu.VMEM((near, 128), F32),
             pltpu.VMEM((far, 128), F32),
-            pltpu.VMEM((2 * pad, near), BF),
-            pltpu.VMEM((2 * pad, far), BF),
-            pltpu.VMEM((hidden, near), BF),
-            pltpu.VMEM((hidden, far), BF),
+            pltpu.VMEM((2 * pad, WHOLE), BF),
+            pltpu.VMEM((2 * pad, far + LEFT), BF),
+            pltpu.VMEM((hidden, WHOLE), BF),
+            pltpu.VMEM((hidden, far + LEFT), BF),
             pltpu.VMEM((2 * pad, 4096), F32),
             pltpu.VMEM((hidden, 4096), F32),
             pltpu.VMEM((3, hidden, 4096), BF),
             pltpu.VMEM((32, 128), F32),
+            pltpu.VMEM((512, 1024), BF),
             pltpu.VMEM((4, PARTS, 64, 1024 // PARTS), BF),
             pltpu.VMEM((3, PARTS, 64, 1024 // PARTS), BF),
             pltpu.VMEM((3, PARTS, 64, 1024 // PARTS), BF),
@@ -693,7 +725,8 @@
             dma((3,)),
             dma((copies,)), dma((copies,)), dma((copies,)), dma((copies,)),
             dma((copies,)), dma((copies,)), dma((copies,)), dma((copies,)),
-            dma((copies,)), dma((copies,)), dma((1,)),
+            dma((copies,)), dma((copies,)),
+            dma((copies,)), dma((copies,)), dma((2,)),
             dma((3, 4)), dma((3, 4)), dma((2,)),
             dma((4, PARTS)), dma((4, PARTS)), dma((3, PARTS)), dma((3, PARTS)),
             dma((8,)), dma((8,)),

time: 118 us -> 111 us (0.941); the launches traced: 117 us -> 111 us
  Pallas kernels: 116 us -> 111 us
    pallas_call x1, Pallas kernels: 112 us -> 107 us  [per_device(): pl.pallas_call(kernel, out_shape=(out, out, out), in_specs=[hbm, hbm, hbm...]
where the time goes in v3:
time: 111 us
  Pallas kernels  111 us (100%)
    pallas_call x1, Pallas kernels, per_device(): pl.pallas_call(kernel, out_shape=(out, out, out), in_specs=[hbm, hbm, hbm...  107 us
    pallas_call x1, Pallas kernels, per_device(): pl.pallas_call(write_kernel, out_shape=(out, out, out), in_specs=[hbm, hb...  3.92 us

profile of v3, /device:TPU:32, one launch (start us, length us, event | category | flops | bytes accessed | tf_op | source)
XLA Modules:
  0.0 111.3 jit_solution(6913681809832769026)
XLA Ops:
  0.6 106.6 %shard_map.121 = (bf16[172,4096]{1,0:T(8,128)(2,1)}, bf16[172,4096]{1,0:T(8,128)(2,1)}, bf16[172,4096]{1,0:T(8,128)(2,1)}) custom-call(bf16[512,1024]{1,0:T(8,128)(2,1)} %bitcast.20, bf16[128,512]{1,0:T(8,128)(2,1)} %context_ref.1, bf16[128,4096]{1,0:T(8,128)(2,1)} %residual_ref.1, bf16[128,4096]{1,0:T(8,128)(2,1)} %cot_ref.1, s32[2,128]{1,0:T(2,128)} %bitcast.21, ...), custom_call_target="tpu_custom_call" | custom-call | tf_op jit(solution)/shard_map/pallas_call | solution.py:683
  107.2 3.9 %shard_map.122 = (bf16[172,4096]{1,0:T(8,128)(2,1)}, bf16[172,4096]{1,0:T(8,128)(2,1)}, bf16[172,4096]{1,0:T(8,128)(2,1)}) custom-call(bf16[172,4096]{1,0:T(8,128)(2,1)} %get-tuple-element.9.refs_0_, bf16[172,4096]{1,0:T(8,128)(2,1)} %get-tuple-element.10.refs_1_, bf16[172,4096]{1,0:T(8,128)(2,1)} %get-tuple-element.11.refs_2_), custom_call_target="tpu_custom_call" | custom-call | tf_op jit(solution)/shard_map/pallas_call | solution.py:745

commit v4 on v3

--- a/solution.py
+++ b/solution.py
@@ -343,7 +343,7 @@
         landed(cot_all.at[rows], ex_recv.at[0, k], ex_send.at[0, k])
         landed(info_all.at[d], ex_recv.at[1, k], ex_send.at[1, k])
 
-    @pl.loop(0, 8)
+    @pl.loop(0, 8, unroll=2)
     def _(e):
         place = (lax.broadcasted_iota(jnp.int32, (160, 128), 0) + e * 160).astype(F32)
         row_gate = jnp.zeros((160, 1), F32)
@@ -450,7 +450,6 @@
     gather_step(3)
     run(cot_far)
     run(cot_near)
-    gather_step(4)
     for qa in RING:
         ctx_gather.from_sibling(qa)
     for k in range(1, 4):
@@ -458,25 +457,38 @@
         landed(res_all.at[rows], ex_recv.at[2, k], ex_send.at[2, k])
     locals_[0].wait()
 
+    last = lax.div(lax.rem(z + 4, 8), 2)
+
+    def feature_product(terms):
+        context = jnp.concatenate(
+            [
+                jnp.concatenate([ctx_all[d * 8 + j, :, pairs] for j, pairs in terms], axis=1)
+                for d in range(4)
+            ],
+            axis=0,
+        )
+        weight = jnp.concatenate([merged_all[j, pairs, :] for j, pairs in terms], axis=0)
+        return jnp.dot(context, weight, preferred_element_type=F32)
+
+    def pair_of(k):
+        return pl.ds(pl.multiple_of(lax.rem(last + k, 4) * 128, 128), 128)
+
+    attn_acc[...] = res_all[...].astype(F32)
+    for j in range(0, 8, 2):
+        attn_acc[...] += feature_product([(j + i, pair_of(k)) for i in range(2) for k in range(1, 4)])
+    gather_step(4)
+
     def lanes(piece):
         return pl.ds(pl.multiple_of(piece * 128, 128), 128)
 
     def gain_of(piece):
         return gain_ref[pl.ds(piece, 1), :]
 
-    for j in range(8):
-        context = jnp.concatenate([ctx_all[d * 8 + j] for d in range(4)], axis=0)
-        product = jnp.dot(context, merged_all[j], preferred_element_type=F32)
-        if j == 0:
-            attn_acc[...] = product + res_all[...].astype(F32)
-        else:
-            attn_acc[...] += product
+    attn_acc[...] += feature_product([(j, pair_of(0)) for j in range(8)])
     res_all[...] = (attn_acc[...] * gain_of(own)).astype(BF)
 
-    @pl.loop(0, 8)
-    def _(e):
-        rows = pl.ds(pl.multiple_of(e * 160, 160), 160)
-        route_x[e] = jnp.dot(sel[rows, :], res_all[...], preferred_element_type=F32).astype(BF)
+    picked = jnp.dot(sel[...], res_all[...], preferred_element_type=F32).astype(BF)
+    route_x[...] = picked.reshape(8, 160, 128)
 
     exchange(route_x, rows_in, tx_send, tx_recv, 0)
 
@@ -582,9 +594,9 @@
     run(cot_near, 2)
     run(cot_far)
     run(cot_near, 2)
-    run(cot_far)
     exchanged(rows_in, tx_send, tx_recv, 0)
     run(in_near)
+    run(cot_far)
     run(cot_own, 4)
     run(cot_far, 3)
     own_back(0, 0, -1, 1, 2)
@@ -614,15 +626,15 @@
     sibling_fore(0, 0)
     run(in_far)
     sibling_fore(0, -1)
-    run(in_far, 2)
+    run(in_far)
     sibling_fore(0, 1)
     sibling_fore(0, 2)
+    activations(0)
+    run(in_far)
+    gradients(0, 0)
     run(in_far, 2)
-    activations(0)
-    gradients(0, 0)
-    run(in_far)
     gradients(0, 1)
-    run(in_far)
+    run(in_far, 2)
     gradients(0, 2)
     gradients(0, 3)
     own_fore(1, 0, -1, 1, 2)

time: 111 us -> 107 us (0.964)
  Pallas kernels: 111 us -> 106 us
    pallas_call x1, Pallas kernels: 107 us -> 102 us  [per_device(): pl.pallas_call(kernel, out_shape=(out, out, out), in_specs=[hbm, hbm, hbm...]
where the time goes in v4:
time: 107 us
  Pallas kernels  106 us (99%)
    pallas_call x1, Pallas kernels, per_device(): pl.pallas_call(kernel, out_shape=(out, out, out), in_specs=[hbm, hbm, hbm...  102 us
    pallas_call x1, Pallas kernels, per_device(): pl.pallas_call(write_kernel, out_shape=(out, out, out), in_specs=[hbm, hb...  3.92 us

profile of v4, /device:TPU:32, one launch (start us, length us, event | category | flops | bytes accessed | tf_op | source)
XLA Modules:
  0.0 106.9 jit_solution(3130876488539134214)
XLA Ops:
  0.6 102.2 %shard_map.121 = (bf16[172,4096]{1,0:T(8,128)(2,1)}, bf16[172,4096]{1,0:T(8,128)(2,1)}, bf16[172,4096]{1,0:T(8,128)(2,1)}) custom-call(bf16[512,1024]{1,0:T(8,128)(2,1)} %bitcast.20, bf16[128,512]{1,0:T(8,128)(2,1)} %context_ref.1, bf16[128,4096]{1,0:T(8,128)(2,1)} %residual_ref.1, bf16[128,4096]{1,0:T(8,128)(2,1)} %cot_ref.1, s32[2,128]{1,0:T(2,128)} %bitcast.21, ...), custom_call_target="tpu_custom_call" | custom-call | tf_op jit(solution)/shard_map/pallas_call | solution.py:695
  102.9 3.9 %shard_map.122 = (bf16[172,4096]{1,0:T(8,128)(2,1)}, bf16[172,4096]{1,0:T(8,128)(2,1)}, bf16[172,4096]{1,0:T(8,128)(2,1)}) custom-call(bf16[172,4096]{1,0:T(8,128)(2,1)} %get-tuple-element.9.refs_0_, bf16[172,4096]{1,0:T(8,128)(2,1)} %get-tuple-element.10.refs_1_, bf16[172,4096]{1,0:T(8,128)(2,1)} %get-tuple-element.11.refs_2_), custom_call_target="tpu_custom_call" | custom-call | tf_op jit(solution)/shard_map/pallas_call | solution.py:757

commit v5 on v4

--- a/solution.py
+++ b/solution.py
@@ -575,7 +575,7 @@
         return jnp.concatenate(pair, axis=1)
 
     def gradients(half, chunk):
-        @pl.loop(0, 4, unroll=2)
+        @pl.loop(0, 4, unroll=4)
         def _(i):
             n = chunk * 4 + i
             cols = pl.ds(pl.multiple_of(n * 256, 256), 256)

time: 107 us -> 105 us (0.981)
  Pallas kernels: 106 us -> 104 us
    pallas_call x1, Pallas kernels: 102 us -> 100 us  [per_device(): pl.pallas_call(kernel, out_shape=(out, out, out), in_specs=[hbm, hbm, hbm...]
where the time goes in v5:
time: 105 us
  Pallas kernels  104 us (99%)
    pallas_call x1, Pallas kernels, per_device(): pl.pallas_call(kernel, out_shape=(out, out, out), in_specs=[hbm, hbm, hbm...  100 us
    pallas_call x1, Pallas kernels, per_device(): pl.pallas_call(write_kernel, out_shape=(out, out, out), in_specs=[hbm, hb...  3.92 us

profile of v5, /device:TPU:32, one launch (start us, length us, event | category | flops | bytes accessed | tf_op | source)
XLA Modules:
  0.0 104.9 jit_solution(1741525266122989597)
XLA Ops:
  0.6 100.2 %shard_map.121 = (bf16[172,4096]{1,0:T(8,128)(2,1)}, bf16[172,4096]{1,0:T(8,128)(2,1)}, bf16[172,4096]{1,0:T(8,128)(2,1)}) custom-call(bf16[512,1024]{1,0:T(8,128)(2,1)} %bitcast.20, bf16[128,512]{1,0:T(8,128)(2,1)} %context_ref.1, bf16[128,4096]{1,0:T(8,128)(2,1)} %residual_ref.1, bf16[128,4096]{1,0:T(8,128)(2,1)} %cot_ref.1, s32[2,128]{1,0:T(2,128)} %bitcast.21, ...), custom_call_target="tpu_custom_call" | custom-call | tf_op jit(solution)/shard_map/pallas_call | solution.py:695
  100.8 3.9 %shard_map.122 = (bf16[172,4096]{1,0:T(8,128)(2,1)}, bf16[172,4096]{1,0:T(8,128)(2,1)}, bf16[172,4096]{1,0:T(8,128)(2,1)}) custom-call(bf16[172,4096]{1,0:T(8,128)(2,1)} %get-tuple-element.9.refs_0_, bf16[172,4096]{1,0:T(8,128)(2,1)} %get-tuple-element.10.refs_1_, bf16[172,4096]{1,0:T(8,128)(2,1)} %get-tuple-element.11.refs_2_), custom_call_target="tpu_custom_call" | custom-call | tf_op jit(solution)/shard_map/pallas_call | solution.py:757
